TPU v7x, 32 devices: a whole 2x2x4 slice. The times are simulated.
32 devices in a mesh: uv: 8 (over y, x, core), tm: 4 (over z).
Axes of the slice: x: 2, y: 2, z: 4, core: 2. Of those that a mesh axis runs over, the one named last changes fastest.
Arguments:
- visibilities: bfloat16 [8, 128, 16384], P(None, 'uv', 'tm'), may hold values from -0.75 to 0.75
- positions: float32 [2, 128, 16384], P(None, 'uv', 'tm'), may hold values from 4 to 60
- owner: int32 [128, 1], P('uv'), may hold values from 0 to 7; in each aligned block of 16 rows (0 to 15, 16 to 31, ...) at most 4 rows name the same one
- w_plane: int32 [128], P('uv'), may hold values from 0 to 7
- row_offset: int32 [128], P('uv'), may hold values from 0 to 127
- col_offset: int32 [128], P('uv'), may hold values from 0 to 1984
Outputs:
- grid: float32 [8, 8, 1024, 2048], P('tm', None, 'uv')
Inputs may be any that keep to these rules, and one draw needn't show every extreme that they name: `owner`: among the 16 subgrids of one index of uv (aligned blocks of rows), no tile is named by more than 4 of them.
All inputs are finite; a program needn't handle non-finite values.
Results may differ from a plain program's by a relative error of at most 0.0037.
Values may be sent and summed in bfloat16 or wider, within the bound.
No kernel may reach another device: no remote copies, remote signals or barrier semaphores. Data moves between devices by JAX's collectives and lax.ppermute only.
A program may use at most 128 MiB of HBM per device.

v0:
```python
import math

import jax
import jax.numpy as jnp
from jax import lax
from jax.sharding import PartitionSpec as P

W = 8
SUB = 64
TAPS = 8
TU = 128
NV = 2048


def passed_along(array, axis, by):
    size = lax.axis_size(axis)
    return lax.ppermute(array, axis, [(i, (i + by) % size) for i in range(size)])


def taper(offsets):
    scaled = offsets * (2.0 / TAPS)
    return jnp.square(jnp.maximum(0.0, 1.0 - scaled * scaled))


def grid_group(values, places):
    comp_count = values.shape[0]
    cell_index = jnp.arange(SUB, dtype=jnp.float32)
    row_taps = taper(cell_index - places[0][:, :, None]).astype(jnp.bfloat16)
    col_taps = taper(cell_index - places[1][:, :, None])
    weighted = (
        jnp.transpose(values, (1, 2, 0)).astype(jnp.float32)[:, :, :, None]
        * col_taps[:, :, None, :]
    )
    weighted = weighted.astype(jnp.bfloat16)
    weighted = weighted.reshape(weighted.shape[0], weighted.shape[1], comp_count * SUB)
    product = jnp.einsum("gpu,gpx->gux", row_taps, weighted, preferred_element_type=jnp.float32)
    product = product.reshape(product.shape[0], SUB, comp_count, SUB)
    return jnp.transpose(product, (2, 0, 1, 3)).reshape(comp_count, product.shape[0], SUB * SUB)


def grid_all(values, places):
    comp_count, sub_count, row_count = values.shape
    span = math.gcd(row_count, 4096)

    def one_group(group_index):
        sub_start = group_index * 4
        group_values = lax.dynamic_slice_in_dim(values, sub_start, 4, 1)
        group_places = lax.dynamic_slice_in_dim(places, sub_start, 4, 1)

        def add_span(step_index, running):
            row_start = step_index * span
            span_values = lax.dynamic_slice_in_dim(group_values, row_start, span, 2)
            span_places = lax.dynamic_slice_in_dim(group_places, row_start, span, 2)
            return running + grid_group(span_values, span_places)

        return lax.fori_loop(
            0, row_count // span, add_span, jnp.zeros((comp_count, 4, SUB * SUB), jnp.float32)
        )

    stacked = lax.map(one_group, jnp.arange(sub_count // 4, dtype=jnp.int32))
    return jnp.transpose(stacked, (1, 0, 2, 3)).reshape(comp_count, sub_count, SUB * SUB)


def fill_slots(subgrids, selector):
    return jnp.einsum("sk,csx->ckx", selector, subgrids, precision=lax.Precision.HIGHEST)


def place_all(arrived, placing_in, row_total, row_base):
    comp_count, slot_count = (arrived.shape[0], arrived.shape[1])
    patches = arrived.reshape(comp_count, slot_count, SUB, SUB)
    anchor = jnp.zeros((), jnp.int32)

    def add_four(turn_index, canvas):
        for inner_index in range(4):
            slot_index = turn_index * 4 + inner_index
            patch_cells = lax.dynamic_index_in_dim(patches, slot_index, 1, keepdims=False)
            plane_index = placing_in[0][slot_index]
            row_start = placing_in[1][slot_index] + row_base
            col_start = placing_in[2][slot_index]
            corner = (anchor, plane_index, row_start, col_start)
            current = lax.dynamic_slice(canvas, corner, (comp_count, 1, SUB, SUB))
            canvas = lax.dynamic_update_slice(canvas, current + patch_cells[:, None], corner)
        return canvas

    canvas = jnp.zeros((comp_count, W, row_total, NV), jnp.float32)
    return lax.fori_loop(0, slot_count // 4, add_four, canvas)


def body(visibilities, positions, owner, w_plane, row_offset, col_offset):
    comps_all, sub_count, row_count = visibilities.shape
    all_places = lax.all_gather(positions, "tm", axis=2, tiled=True)
    my_values = lax.all_to_all(visibilities, "tm", split_axis=0, concat_axis=2, tiled=True)
    subgrids = grid_all(my_values, all_places)
    peers = lax.axis_size("uv")
    capacity = 2 * sub_count // peers
    target = owner[:, 0]
    member = (target[:, None] == jnp.arange(peers, dtype=jnp.int32)[None, :]).astype(jnp.int32)
    earlier = jnp.cumsum(member, axis=0) - member
    slot_rank = jnp.sum(earlier * member, axis=1)
    placing = jnp.stack([w_plane, row_offset, col_offset], axis=0)
    slot_count = peers * capacity
    destination = target * capacity + slot_rank
    slot_ids = jnp.arange(slot_count, dtype=jnp.int32)
    chosen = (destination[:, None] == slot_ids[None, :]).astype(jnp.int32)
    outgoing = fill_slots(subgrids, chosen.astype(jnp.float32))
    placing_out = jnp.sum(placing[:, :, None] * chosen[None], axis=1)
    arrived, placing_in = (
        lax.all_to_all(outgoing, "uv", split_axis=1, concat_axis=1, tiled=True),
        lax.all_to_all(placing_out, "uv", split_axis=1, concat_axis=1, tiled=True),
    )
    extended = place_all(arrived, placing_in, TU + SUB, 0)
    spill_rows = extended[:, :, TU:, :]
    incoming = passed_along(spill_rows, "uv", 1)
    tile_grid = extended[:, :, :TU, :]
    return tile_grid.at[:, :, :SUB, :].add(incoming)


def solution(mesh):
    placed = (P(None, "uv", "tm"), P(None, "uv", "tm"), P("uv", None), P("uv"), P("uv"), P("uv"))
    return jax.shard_map(
        body, mesh=mesh, in_specs=placed, out_specs=P("tm", None, "uv", None), check_vma=False
    )
```

profile of v0, /device:TPU:0, one launch (start us, length us, event | category | flops | bytes accessed | tf_op | source)
XLA Modules:
  0.0 624.4 jit_solution(2184081551056787463)
XLA Ops:
  7.3 6.3 %all-to-all-start.1 = ((bf16[8,16,4096]{2,1,0:T(8,128)(2,1)}), bf16[8,16,4096]{2,1,0:T(8,128)(2,1)S(1)}, u32[]{:S(2)}, u32[]{:S(2)}) async-start(bf16[8,16,4096]{2,1,0:T(8,128)(2,1)} %param.14), calls=%async_computation.1 | async-start | bytes 2097152 | tf_op jit(solution)/shard_map/all_to_all | solution.py:92
  17.9 45.0 %all-to-all-done.1 = bf16[8,16,4096]{2,1,0:T(8,128)(2,1)S(1)} async-done(((bf16[8,16,4096]{2,1,0:T(8,128)(2,1)}), bf16[8,16,4096]{2,1,0:T(8,128)(2,1)S(1)}, u32[]{:S(2)}, u32[]{:S(2)}) %all-to-all-start.1) | async-done | bytes 1048608 | tf_op jit(solution)/shard_map/all_to_all | solution.py:92
  62.9 3.9 all-to-all-start
  68.8 4.8 all-gather.2.cloned.1.call-done
  73.5 73.4 %while.41 = (s32[]{:T(128)}, f32[4,2,4,4096]{3,2,1,0:T(4,128)S(1)}, s32[4]{0:T(128)S(1)}, bf16[2,16,16384]{2,0,1:T(2,128)(2,1)S(1)}, f32[2,16,16384]{2,1,0:T(8,1...) while((s32[]{:T(128)}, f32[4,2,4,4096]{3,2,1,0:T(4,128)S(1)}, ...), condition=%wide.region_3.4_spmd, body=%wide.region_0.3_spmd.sunk | while | flops 286359552 | bytes 20644312 | solution.py:60
  76.3 15.6 %while.43 = (s32[]{:T(128)}, f32[2,4,4096]{2,1,0:T(4,128)S(1)}, f32[2,4,16384]{2,1,0:T(4,128)S(1)}, bf16[2,4,16384]{2,0,1:T(2,128)(2,1)S(1)}, s32[]{:T(128)}, /*index=5*/s32[]{:T(128)}, s32[]{:T(128)}, s32[]{:T(128)}, s32[]{}) while((s32[]{:T(128)}, f32[2,4,4096]{2,1,0:T(4,128)S(1)}, f32[2,4,16384]{2,1,0:T(4,128)S(1)}, ...), condition=%wide.region_2.2_spmd.clone, body=%wide.region_1.1_spmd.clone.sunk | while | flops 286359552 | bytes 18809012 | solution.py:56
  94.7 15.6 %while.43 = (s32[]{:T(128)}, f32[2,4,4096]{2,1,0:T(4,128)S(1)}, f32[2,4,16384]{2,1,0:T(4,128)S(1)}, bf16[2,4,16384]{2,0,1:T(2,128)(2,1)S(1)}, s32[]{:T(128)}, /*index=5*/s32[]{:T(128)}, s32[]{:T(128)}, s32[]{:T(128)}, s32[]{}) while((s32[]{:T(128)}, f32[2,4,4096]{2,1,0:T(4,128)S(1)}, f32[2,4,16384]{2,1,0:T(4,128)S(1)}, ...), condition=%wide.region_2.2_spmd.clone, body=%wide.region_1.1_spmd.clone.sunk | while | flops 286359552 | bytes 18809012 | solution.py:56
  113.0 15.6 %while.43 = (s32[]{:T(128)}, f32[2,4,4096]{2,1,0:T(4,128)S(1)}, f32[2,4,16384]{2,1,0:T(4,128)S(1)}, bf16[2,4,16384]{2,0,1:T(2,128)(2,1)S(1)}, s32[]{:T(128)}, /*index=5*/s32[]{:T(128)}, s32[]{:T(128)}, s32[]{:T(128)}, s32[]{}) while((s32[]{:T(128)}, f32[2,4,4096]{2,1,0:T(4,128)S(1)}, f32[2,4,16384]{2,1,0:T(4,128)S(1)}, ...), condition=%wide.region_2.2_spmd.clone, body=%wide.region_1.1_spmd.clone.sunk | while | flops 286359552 | bytes 18809012 | solution.py:56
  131.4 15.6 %while.43 = (s32[]{:T(128)}, f32[2,4,4096]{2,1,0:T(4,128)S(1)}, f32[2,4,16384]{2,1,0:T(4,128)S(1)}, bf16[2,4,16384]{2,0,1:T(2,128)(2,1)S(1)}, s32[]{:T(128)}, /*index=5*/s32[]{:T(128)}, s32[]{:T(128)}, s32[]{:T(128)}, s32[]{}) while((s32[]{:T(128)}, f32[2,4,4096]{2,1,0:T(4,128)S(1)}, f32[2,4,16384]{2,1,0:T(4,128)S(1)}, ...), condition=%wide.region_2.2_spmd.clone, body=%wide.region_1.1_spmd.clone.sunk | while | flops 286359552 | bytes 18809012 | solution.py:56
  150.5 3.7 all-to-all-start.2
  155.0 14.6 %all-to-all-done.2 = f32[2,32,4096]{2,0,1:T(2,128)S(1)} async-done(((f32[2,32,4096]{2,0,1:T(2,128)}), f32[2,32,4096]{2,0,1:T(2,128)S(1)}, u32[]{:S(2)}, u32[]{:S(2)}) %all-to-all-start.2) | async-done | bytes 1048608 | tf_op jit(solution)/shard_map/all_to_all | solution.py:108
  172.3 11.5 %broadcast_in_dim.18 = f32[2,8,192,2048]{3,2,1,0:T(8,128)} broadcast(f32[]{:T(128)} %constant.252.clone.1), dimensions={} | broadcast | bytes 25165828 | tf_op jit(solution)/shard_map/broadcast_in_dim | solution.py:85
  183.8 324.0 %while.42 = (s32[]{:T(128)}, f32[2,8,192,2048]{3,2,1,0:T(8,128)}, s32[3,32]{1,0:T(4,128)S(1)}, f32[2,32,64,64]{3,2,1,0:T(8,128)}, s32[]{:T(128)}, /*index=5*/s32...) while((s32[]{:T(128)}, f32[2,8,192,2048]{3,2,1,0:T(8,128)}, ...), condition=%wide.region_8.9_spmd, body=%wide.region_7.8_spmd.sunk | while | flops 32822 | bytes 657077 | solution.py:86
  208.4 3.4 dynamic_update_slice.51
  212.8 3.4 dynamic_update_slice.52
  330.0 3.4 dynamic_update_slice.51
  370.5 3.4 dynamic_update_slice.51
  374.9 3.4 dynamic_update_slice.52
  455.8 3.4 dynamic_update_slice.52
  496.2 3.4 dynamic_update_slice.52
  507.8 4.0 slice.91
  511.8 11.8 %slice.89 = f32[2,8,128,2048]{3,2,1,0:T(8,128)} slice(f32[2,8,192,2048]{3,2,1,0:T(8,128)} %get-tuple-element.236), slice={[0:2], [0:8], [0:128], [0:2048]} | slice | bytes 33554432 | tf_op jit(solution)/shard_map/slice | solution.py:114
  523.6 82.0 %collective-permute-done = f32[2,8,64,2048]{3,2,1,0:T(8,128)} collective-permute-done((f32[2,8,64,2048]{3,2,1,0:T(8,128)S(1)}, f32[2,8,64,2048]{3,2,1,0:T(8,128)}, u32[]{:S(2)}, u32[]{:S(2)}) %collective-permute-start) | collective-permute-done | bytes 8388640 | tf_op jit(solution)/shard_map/ppermute | solution.py:17
  605.7 11.9 %add_dynamic-update-slice_fusion = f32[2,8,128,2048]{3,2,1,0:T(8,128)} fusion(f32[2,8,128,2048]{3,2,1,0:T(8,128)} %slice.89, f32[2,8,64,2048]{3,2,1,0:T(8,128)} %collective-permute-done, f32[2,8,192,2048]{3,2,1,0:T(8,128)} %get-tuple-element.236), kind=kLoop, calls=%fused_computation.34 | loop fusion | flops 2097152 | bytes 25165824 | tf_op jit(solution)/shard_map/scatter-add | solution.py:115
  (273 shorter events, 206.0 us)
Async XLA Ops:
  6.5 67.0 %all-gather.2.cloned.1.call-start = ((), (), s32[]{:S(2)}) async-start(), calls=%async_computation.3 | async-start | bytes 2621440 | tf_op jit(solution)/shard_map/all_gather | solution.py:91
  7.3 55.6 %all-to-all-start.1 = ((bf16[8,16,4096]{2,1,0:T(8,128)(2,1)}), bf16[8,16,4096]{2,1,0:T(8,128)(2,1)S(1)}, u32[]{:S(2)}, u32[]{:S(2)}) async-start(bf16[8,16,4096]{2,1,0:T(8,128)(2,1)} %param.14), calls=%async_computation.1 | async-start | bytes 2097152 | tf_op jit(solution)/shard_map/all_to_all | solution.py:92
  16.5 0.5 copy-start
  62.9 87.6 %all-to-all-start = ((s32[3,8,4]{2,0,1:T(4,128)}), s32[3,8,4]{2,0,1:T(4,128)}, u32[]{:S(2)}, u32[]{:S(2)}) async-start(s32[3,8,4]{2,0,1:T(4,128)} %copy.26), calls=%async_computation | async-start | bytes 32768 | tf_op jit(solution)/shard_map/all_to_all | solution.py:109
  73.5 73.9 %copy-start.1 = (s32[16]{0:T(128)S(1)}, s32[16]{0:T(128)}, u32[]{:S(2)}) copy-start(s32[16]{0:T(128)} %copy-done) | copy-start | bytes 196
  150.5 19.1 %all-to-all-start.2 = ((f32[2,32,4096]{2,0,1:T(2,128)}), f32[2,32,4096]{2,0,1:T(2,128)S(1)}, u32[]{:S(2)}, u32[]{:S(2)}) async-start(f32[2,32,4096]{2,0,1:T(2,128)} %copy.31), calls=%async_computation.2 | async-start | bytes 2097152 | tf_op jit(solution)/shard_map/all_to_all | solution.py:108
  511.7 93.9 %collective-permute-start = (f32[2,8,64,2048]{3,2,1,0:T(8,128)S(1)}, f32[2,8,64,2048]{3,2,1,0:T(8,128)}, u32[]{:S(2)}, u32[]{:S(2)}) collective-permute-start(f32[2,8,64,2048]{3,2,1,0:T(8,128)S(1)} %slice.91), channel_id=1, source_target_pairs={{0,4},{4,8},{8,12},{12,16},{16,20},{20,24},{24,28},{28,0},{1,5},{5... | collective-permute-start | bytes 25165832 | tf_op jit(solution)/shard_map/ppermute | solution.py:17
Sparse Core Ops, SparseCore 0:
  8.9 64.5 all-gather.1
where the time goes:
time: 634 us; the launch traced here: 624 us
  loops' own time  182 us (29%)
  local copies, waits for them, and re-layouts  163 us (26%)
  waiting for transfers between devices  147 us (23%)
  other arithmetic  78 us (12%)
  matrix products  26.7 us (4%)
  starting transfers between devices  14.1 us (2%)
  between operations  13.5 us (2%)
    another operation x1, loops' own time, place_all(): return lax.fori_loop(0, slot_count // 4, add_four, canvas)  178 us
    dynamic_update_slice x32, local copies, waits for them, and re-layouts, add_four(): lax.dynamic_update_slice(canvas, current + patch_cells[:, None], corner)  102 us
    ppermute x1, waiting for transfers between devices, passed_along(): lax.ppermute(array, axis, [(i, (i + by) % size) for i in range(size)])  82 us
    all_to_all x1, waiting for transfers between devices, body(): lax.all_to_all(visibilities, 'tm', split_axis=0, concat_axis=2, tiled=True)  45 us
    add x32, other arithmetic, add_four(): current + patch_cells[:, None]  33.3 us
    dot_general x16, matrix products, grid_group(): jnp.einsum('gpu,gpx->gux', row_taps, weighted, preferred_element_type=jnp...  25.4 us
    all_to_all x1, waiting for transfers between devices, body(): lax.all_to_all(outgoing, 'uv', split_axis=1, concat_axis=1, tiled=True)  14.6 us
    square x16, other arithmetic, taper(): return jnp.square(jnp.maximum(0.0, 1.0 - scaled * scaled))  13.2 us
  transfers between devices with their start and end apart: 5, of which 4 were waited for; matrix products, arithmetic and copies ran while one was open for 14% of the time, Pallas kernels for 0%

commit v1 on v0

v1 whole, which is shorter than its diff:
```python
import functools

import jax
import jax.numpy as jnp
from jax import lax
from jax.experimental import pallas as pl
from jax.experimental.pallas import tpu as pltpu
from jax.sharding import PartitionSpec as P

W = 8
SUB = 64
TAPS = 8
TU = 128
NV = 2048
LANES = 128
SUBLANES = 8


def taper(scaled):
    inner = jnp.maximum(0.0, 1.0 - scaled * scaled)
    return inner * inner


def grid_kernel(values_ref, places_ref, parts_ref, values_wide, *, peers):
    comp_count, sub_count, row_count = values_ref.shape
    kept = parts_ref.shape[3]
    for comp in range(comp_count):
        values_wide[comp * sub_count : (comp + 1) * sub_count, :] = values_ref[comp].astype(jnp.float32)
    cells = lax.broadcasted_iota(jnp.int32, (SUB, row_count), 0).astype(jnp.float32) * (2.0 / TAPS)

    def one_sub(sub, carry):
        row_taps = taper(cells - places_ref[0, pl.ds(sub, 1), :] * (2.0 / TAPS)).astype(jnp.bfloat16)
        col_taps = taper(cells - places_ref[1, pl.ds(sub, 1), :] * (2.0 / TAPS))
        weighted = jnp.concatenate(
            [
                (values_wide[pl.ds(comp * sub_count + sub, 1), :] * col_taps).astype(jnp.bfloat16)
                for comp in range(comp_count)
            ],
            axis=0,
        )
        cellsums = lax.dot_general(
            row_taps, weighted, (((1,), (1,)), ((), ())), preferred_element_type=jnp.float32
        ).astype(jnp.bfloat16)
        for peer in range(peers):
            parts_ref[peer, sub] = cellsums[:, peer * kept : (peer + 1) * kept]
        return carry

    lax.fori_loop(0, sub_count, one_sub, 0)


def grid_parts(values, places, peers):
    comp_count, sub_count, row_count = values.shape
    kept = comp_count // peers * SUB
    return pl.pallas_call(
        functools.partial(grid_kernel, peers=peers),
        out_shape=jax.ShapeDtypeStruct((peers, sub_count, SUB, kept), jnp.bfloat16),
        in_specs=[pl.BlockSpec(memory_space=pltpu.VMEM)] * 2,
        out_specs=pl.BlockSpec(memory_space=pltpu.VMEM),
        scratch_shapes=[pltpu.VMEM((comp_count * sub_count, row_count), jnp.float32)],
        compiler_params=pltpu.CompilerParams(vmem_limit_bytes=48 << 20),
        cost_estimate=pl.CostEstimate(
            flops=2 * sub_count * row_count * SUB * SUB * comp_count,
            bytes_accessed=4 << 20,
            transcendentals=0,
        ),
    )(values, places)


def place_kernel(start_ref, plane_ref, col_ref, patches_ref, out_ref, canvas, sem, count, listed):
    total = start_ref.shape[0]
    comp_count = canvas.shape[1]
    for plane in range(W):
        count[plane] = 0

    def enlist(sub, carry):
        @pl.when(start_ref[sub] >= 0)
        def _():
            plane = plane_ref[sub]
            at = count[plane]
            listed[plane, at] = sub
            count[plane] = at + 1

        return carry

    lax.fori_loop(0, total, enlist, 0)
    lane = lax.broadcasted_iota(jnp.int32, (SUB + SUBLANES, LANES), 1)

    def out_copy(slot, plane):
        return pltpu.make_async_copy(
            canvas.at[slot, :, pl.ds(SUB, TU), :], out_ref.at[:, plane], sem.at[slot]
        )

    def one_plane(plane, slot):
        canvas[slot] = jnp.zeros(canvas.shape[1:], jnp.float32)

        def add_patch(index, carry):
            sub = listed[plane, index]
            start = start_ref[sub]
            col = col_ref[sub]
            block = pl.multiple_of(col // LANES * LANES, LANES)
            shift = col % LANES
            patch = patches_ref[sub].astype(jnp.float32)
            if patch.shape[1] < LANES:
                patch = jnp.concatenate([patch] * (LANES // patch.shape[1]), axis=1)
            patch = jnp.concatenate([patch, jnp.zeros((SUBLANES, patch.shape[1]), jnp.float32)], axis=0)
            patch = pltpu.roll(patch, start % SUBLANES, 0)
            rows = pl.ds(pl.multiple_of(start // SUBLANES * SUBLANES, SUBLANES), SUB + SUBLANES)
            for comp in range(comp_count):
                source = patch[:, comp // 2 * LANES : (comp // 2 + 1) * LANES]
                turned = pltpu.roll(source, (shift + comp % 2 * SUB) % LANES, 1)
                here = (lane >= shift) & (lane < shift + SUB)
                canvas[slot, comp, rows, pl.ds(block, LANES)] += jnp.where(here, turned, 0.0)

                @pl.when(shift > LANES - SUB)
                def _():
                    canvas[slot, comp, rows, pl.ds(block + LANES, LANES)] += jnp.where(
                        lane < shift + SUB - LANES, turned, 0.0
                    )

            return carry

        lax.fori_loop(0, count[plane], add_patch, 0)
        out_copy(slot, plane).start()

    for plane in range(W):
        slot = plane % 2
        if plane >= 2:
            out_copy(slot, plane - 2).wait()
        one_plane(plane, slot)
    for plane in range(W - 2, W):
        out_copy(plane % 2, plane).wait()


def place_all(patches, starts, planes, cols, comp_count):
    total = patches.shape[0]
    smem = pl.BlockSpec(memory_space=pltpu.SMEM)
    return pl.pallas_call(
        place_kernel,
        out_shape=jax.ShapeDtypeStruct((comp_count, W, TU, NV), jnp.float32),
        in_specs=[smem, smem, smem, pl.BlockSpec(memory_space=pltpu.VMEM)],
        out_specs=pl.BlockSpec(memory_space=pl.ANY),
        scratch_shapes=[
            pltpu.VMEM((2, comp_count, TU + 2 * SUB, NV), jnp.float32),
            pltpu.SemaphoreType.DMA((2,)),
            pltpu.SMEM((W,), jnp.int32),
            pltpu.SMEM((W, total), jnp.int32),
        ],
        compiler_params=pltpu.CompilerParams(vmem_limit_bytes=32 << 20),
        cost_estimate=pl.CostEstimate(
            flops=0, bytes_accessed=comp_count * W * TU * NV * 4, transcendentals=0
        ),
    )(starts, planes, cols, patches)


def gather_around(array, axis):
    size = lax.axis_size(axis)
    hops = [array] + [
        lax.ppermute(array, axis, [((i + by) % size, i) for i in range(size)]) for by in range(1, size)
    ]
    return jnp.stack(hops, axis=0)


def body(visibilities, positions, owner, w_plane, row_offset, col_offset):
    peers = lax.axis_size("tm")
    tiles = lax.axis_size("uv")
    comp_count = visibilities.shape[0] // peers
    tile = lax.axis_index("uv")
    parts = grid_parts(visibilities, positions, peers)
    swapped = lax.all_to_all(parts, "tm", split_axis=0, concat_axis=0, tiled=True)
    summed = jnp.sum(swapped.astype(jnp.float32), axis=0).astype(jnp.bfloat16)
    patches = gather_around(summed, "uv")
    patches = patches.reshape((-1,) + patches.shape[2:])
    placing = gather_around(jnp.stack([owner[:, 0], row_offset, w_plane, col_offset], axis=0), "uv")
    placing = jnp.transpose(placing, (1, 0, 2)).reshape(4, -1)
    ahead = (placing[0] - tile) % tiles
    starts = jnp.where(ahead == 0, placing[1] + SUB, jnp.where(ahead == tiles - 1, placing[1] + SUB - TU, -1))
    return place_all(patches, starts, placing[2], placing[3], comp_count)


def solution(mesh):
    placed = (P(None, "uv", "tm"), P(None, "uv", "tm"), P("uv", None), P("uv"), P("uv"), P("uv"))
    return jax.shard_map(
        body, mesh=mesh, in_specs=placed, out_specs=P("tm", None, "uv", None), check_vma=False
    )
```

time: 634 us -> 110 us (0.17); the launches traced: 624 us -> 108 us
  loops' own time: 182 us -> 0 us
  local copies, waits for them, and re-layouts: 163 us -> 3 us
  waiting for transfers between devices: 147 us -> 47.9 us
  other arithmetic: 78 us -> 0.99 us
  Pallas kernels: 0 us -> 36.8 us
  matrix products: 26.7 us -> 0 us
  between operations: 13.5 us -> 0.18 us
    another operation x6 -> x0, loops' own time: 182 us -> none  [the longest x1 178 us: place_all(): return lax.fori_loop(0, slot_count // 4, add_four, canvas)]
    dynamic_update_slice x36 -> x0, local copies, waits for them, and re-layouts: 102 us -> none  [the longest x32 102 us: add_four(): lax.dynamic_update_slice(canvas, current + patch_cells[:, None], corner)]
    ppermute x1 -> x14, waiting for transfers between devices: 82 us -> 30.1 us  [gather_around(): lax.ppermute(array, axis, [((i + by) % size, i) for i in range(size)])]
    all_to_all x3 -> x1, waiting for transfers between devices: 59.6 us -> 17.8 us  [body(): lax.all_to_all(parts, 'tm', split_axis=0, concat_axis=0, tiled=True)]
    pallas_call x0 -> x2, Pallas kernels: none -> 36.8 us  [the longest x1 23.9 us: grid_parts(): pl.pallas_call(functools.partial(grid_kernel, peers=peers), out_shape=jax...]
    add x48 -> x0, other arithmetic: 36 us -> none  [the longest x32 33.3 us: add_four(): current + patch_cells[:, None]]
    dot_general x17 -> x0, matrix products: 26.7 us -> none  [the longest x16 25.4 us: grid_group(): jnp.einsum('gpu,gpx->gux', row_taps, weighted, preferred_element_type=jnp...]
    dynamic_slice x28 -> x0, local copies, waits for them, and re-layouts: 19.4 us -> none  [the longest x8 5.5 us: add_four(): col_start = placing_in[2][slot_index]]
  transfers between devices with their start and end apart: 5 -> 15, of which waited for: 4 -> 7; matrix products, arithmetic and copies ran while one was open for 14% -> 1% of each run, Pallas kernels for 0% -> 22%
where the time goes in v1:
time: 110 us; the launch traced here: 108 us
  waiting for transfers between devices  47.9 us (44%)
  Pallas kernels  36.8 us (33%)
  starting transfers between devices  19.2 us (17%)
  local copies, waits for them, and re-layouts  3 us (3%)
    ppermute x14, waiting for transfers between devices, gather_around(): lax.ppermute(array, axis, [((i + by) % size, i) for i in range(size)])  30.1 us
    pallas_call x1, Pallas kernels, grid_parts(): pl.pallas_call(functools.partial(grid_kernel, peers=peers), out_shape=jax...  23.9 us
    all_to_all x1, waiting for transfers between devices, body(): lax.all_to_all(parts, 'tm', split_axis=0, concat_axis=0, tiled=True)  17.8 us
    ppermute x14, starting transfers between devices, gather_around(): lax.ppermute(array, axis, [((i + by) % size, i) for i in range(size)])  14.2 us
    pallas_call x1, Pallas kernels, place_all(): pl.pallas_call(place_kernel, out_shape=jax.ShapeDtypeStruct((comp_count,...  12.9 us
    all_to_all x1, starting transfers between devices, body(): lax.all_to_all(parts, 'tm', split_axis=0, concat_axis=0, tiled=True)  5.02 us
    unnamed x25, local copies, waits for them, and re-layouts  2.56 us
  transfers between devices with their start and end apart: 15, of which 7 were waited for; matrix products, arithmetic and copies ran while one was open for 1% of the time, Pallas kernels for 22%

profile of v1, /device:TPU:0, one launch (start us, length us, event | category | flops | bytes accessed | tf_op | source)
XLA Modules:
  0.0 108.1 jit_solution(13982167096031890585)
XLA Ops:
  0.0 0.7 pad_add_fusion
  0.7 3.0 %collective-permute-start.5 = (s32[4,16]{1,0:T(4,128)S(1)}, s32[4,16]{1,0:T(4,128)S(1)}, u32[]{:S(2)}, u32[]{:S(2)}) collective-permute-start(s32[4,16]{1,0:T(4,128)S(1)} %pad_add_fusion), channel_id=1, source_target_pairs={{24,0},{28,4},{0,8},{4,12},{8,16},{12,20},{16,24},{20,28},{25,1},{... | collective-permute-start | bytes 776 | tf_op jit(solution)/shard_map/ppermute | solution.py:158
  3.7 0.7 collective-permute-start.4
  4.3 0.9 collective-permute-start.3
  5.3 1.4 %collective-permute-start.2 = (s32[4,16]{1,0:T(4,128)S(1)}, s32[4,16]{1,0:T(4,128)S(1)}, u32[]{:S(2)}, u32[]{:S(2)}) collective-permute-start(s32[4,16]{1,0:T(4,128)S(1)} %pad_add_fusion), channel_id=1, source_target_pairs={{12,0},{16,4},{20,8},{24,12},{28,16},{0,20},{4,24},{8,28},{13,1},{... | collective-permute-start | bytes 776 | tf_op jit(solution)/shard_map/ppermute | solution.py:158
  6.7 0.9 collective-permute-start
  7.6 1.2 %copy-done = bf16[8,16,4096]{2,1,0:T(8,128)(2,1)S(1)} copy-done((bf16[8,16,4096]{2,1,0:T(8,128)(2,1)S(1)}, bf16[8,16,4096]{2,1,0:T(8,128)(2,1)}, u32[]{:S(2)}) %copy-start) | copy-done | bytes 1048600
  8.8 1.0 copy-done.1
  9.8 23.9 %shard_map.64 = bf16[4,16,64,128]{3,2,1,0:T(8,128)(2,1)} custom-call(bf16[8,16,4096]{2,1,0:T(8,128)(2,1)S(1)} %copy-done, f32[2,16,4096]{2,1,0:T(8,128)S(1)} %copy-done.1), custom_call_target="tpu_custom_call" | custom-call | flops 4294967296 | bytes 4194304 | tf_op jit(solution)/shard_map/pallas_call | solution.py:54
  33.7 5.0 %all-to-all-start = ((bf16[4,16,64,128]{3,2,1,0:T(8,128)(2,1)}), bf16[4,16,64,128]{3,2,1,0:T(8,128)(2,1)S(1)}, u32[]{:S(2)}, u32[]{:S(2)}) async-start(bf16[4,16,64,128]{3,2,1,0:T(8,128)(2,1)} %shard_map.64), calls=%async_computation | async-start | bytes 2097152 | tf_op jit(solution)/shard_map/all_to_all | solution.py:169
  38.8 1.5 %collective-permute-start.1 = (s32[4,16]{1,0:T(4,128)S(1)}, s32[4,16]{1,0:T(4,128)S(1)}, u32[]{:S(2)}, u32[]{:S(2)}) collective-permute-start(s32[4,16]{1,0:T(4,128)S(1)} %pad_add_fusion), channel_id=1, source_target_pairs={{8,0},{12,4},{16,8},{20,12},{24,16},{28,20},{0,24},{4,28},{9,1},{1... | collective-permute-start | bytes 776 | tf_op jit(solution)/shard_map/ppermute | solution.py:158
  40.3 2.1 %collective-permute-done.1 = s32[4,16]{1,0:T(4,128)S(1)} collective-permute-done((s32[4,16]{1,0:T(4,128)S(1)}, s32[4,16]{1,0:T(4,128)S(1)}, u32[]{:S(2)}, u32[]{:S(2)}) %collective-permute-start.1) | collective-permute-done | bytes 288 | tf_op jit(solution)/shard_map/ppermute | solution.py:158
  42.5 3.8 %collective-permute-done.6 = s32[4,16]{1,0:T(4,128)S(1)} collective-permute-done((s32[4,16]{1,0:T(4,128)S(1)}, s32[4,16]{1,0:T(4,128)S(1)}, u32[]{:S(2)}, u32[]{:S(2)}) %collective-permute-start.6) | collective-permute-done | bytes 288 | tf_op jit(solution)/shard_map/ppermute | solution.py:158
  46.7 17.8 %all-to-all-done = bf16[4,16,64,128]{3,2,1,0:T(8,128)(2,1)S(1)} async-done(((bf16[4,16,64,128]{3,2,1,0:T(8,128)(2,1)}), bf16[4,16,64,128]{3,2,1,0:T(8,128)(2,1)S(1)}, u32[]{:S(2)}, u32[]{:S(2)}) %all-to-all-start) | async-done | bytes 1048608 | tf_op jit(solution)/shard_map/all_to_all | solution.py:169
  64.9 0.5 collective-permute-start.13
  65.7 1.9 %collective-permute-start.11 = (bf16[16,64,128]{2,1,0:T(8,128)(2,1)S(1)}, bf16[16,64,128]{2,1,0:T(8,128)(2,1)S(1)}, u32[]{:S(2)}, u32[]{:S(2)}) collective-permute-start(bf16[16,64,128]{2,1,0:T(8,128)(2,1)S(1)} %reduce_sum.12), channel_id=1, source_target_pairs={{20,0},{24,4},{28,8},{0,12},{4,16},{8,20},{12,24},{16,28},{21,1},{... | collective-permute-start | bytes 786440 | tf_op jit(solution)/shard_map/ppermute | solution.py:158
  67.6 1.7 %collective-permute-start.8 = (bf16[16,64,128]{2,1,0:T(8,128)(2,1)S(1)}, bf16[16,64,128]{2,1,0:T(8,128)(2,1)S(1)}, u32[]{:S(2)}, u32[]{:S(2)}) collective-permute-start(bf16[16,64,128]{2,1,0:T(8,128)(2,1)S(1)} %reduce_sum.12), channel_id=1, source_target_pairs={{8,0},{12,4},{16,8},{20,12},{24,16},{28,20},{0,24},{4,28},{9,1},{1... | collective-permute-start | bytes 786440 | tf_op jit(solution)/shard_map/ppermute | solution.py:158
  69.3 1.9 %collective-permute-done.7 = bf16[16,64,128]{2,1,0:T(8,128)(2,1)S(1)} collective-permute-done((bf16[16,64,128]{2,1,0:T(8,128)(2,1)S(1)}, bf16[16,64,128]{2,1,0:T(8,128)(2,1)S(1)}, u32[]{:S(2)}, u32[]{:S(2)}) %collective-permute-start.7) | collective-permute-done | bytes 262176 | tf_op jit(solution)/shard_map/ppermute | solution.py:158
  71.2 0.9 collective-permute-start.9
  72.1 16.6 %collective-permute-done.8 = bf16[16,64,128]{2,1,0:T(8,128)(2,1)S(1)} collective-permute-done((bf16[16,64,128]{2,1,0:T(8,128)(2,1)S(1)}, bf16[16,64,128]{2,1,0:T(8,128)(2,1)S(1)}, u32[]{:S(2)}, u32[]{:S(2)}) %collective-permute-start.8) | collective-permute-done | bytes 262176 | tf_op jit(solution)/shard_map/ppermute | solution.py:158
  88.6 0.6 collective-permute-start.10
  89.2 0.3 collective-permute-done.9
  89.5 5.4 %collective-permute-done.10 = bf16[16,64,128]{2,1,0:T(8,128)(2,1)S(1)} collective-permute-done((bf16[16,64,128]{2,1,0:T(8,128)(2,1)S(1)}, bf16[16,64,128]{2,1,0:T(8,128)(2,1)S(1)}, u32[]{:S(2)}, u32[]{:S(2)}) %collective-permute-start.10) | collective-permute-done | bytes 262176 | tf_op jit(solution)/shard_map/ppermute | solution.py:158
  95.2 12.9 %shard_map.65 = f32[2,8,128,2048]{3,2,1,0:T(8,128)} custom-call(s32[128]{0:T(128)S(1)} %compare_select_fusion.3.start_ref, s32[128]{0:T(128)S(1)} %squeeze.4.plane_ref, s32[128]{0:T(128)S(1)} %squeeze.10.col_ref, bf16[128,64,128]{2,1,0:T(8,128)(2,1)S(1)} %bitcast.38), custom_call_target="tpu_custom_call" | custom-call | bytes 16777216 | tf_op jit(solution)/shard_map/pallas_call | solution.py:137
  (45 shorter events, 1.3 us)
Async XLA Ops:
  0.7 41.8 %collective-permute-start.5 = (s32[4,16]{1,0:T(4,128)S(1)}, s32[4,16]{1,0:T(4,128)S(1)}, u32[]{:S(2)}, u32[]{:S(2)}) collective-permute-start(s32[4,16]{1,0:T(4,128)S(1)} %pad_add_fusion), channel_id=1, source_target_pairs={{24,0},{28,4},{0,8},{4,12},{8,16},{12,20},{16,24},{20,28},{25,1},{... | collective-permute-start | bytes 776 | tf_op jit(solution)/shard_map/ppermute | solution.py:158
  3.7 38.8 %collective-permute-start.4 = (s32[4,16]{1,0:T(4,128)S(1)}, s32[4,16]{1,0:T(4,128)S(1)}, u32[]{:S(2)}, u32[]{:S(2)}) collective-permute-start(s32[4,16]{1,0:T(4,128)S(1)} %pad_add_fusion), channel_id=1, source_target_pairs={{20,0},{24,4},{28,8},{0,12},{4,16},{8,20},{12,24},{16,28},{21,1},{... | collective-permute-start | bytes 776 | tf_op jit(solution)/shard_map/ppermute | solution.py:158
  4.3 38.1 %collective-permute-start.3 = (s32[4,16]{1,0:T(4,128)S(1)}, s32[4,16]{1,0:T(4,128)S(1)}, u32[]{:S(2)}, u32[]{:S(2)}) collective-permute-start(s32[4,16]{1,0:T(4,128)S(1)} %pad_add_fusion), channel_id=1, source_target_pairs={{16,0},{20,4},{24,8},{28,12},{0,16},{4,20},{8,24},{12,28},{17,1},{... | collective-permute-start | bytes 776 | tf_op jit(solution)/shard_map/ppermute | solution.py:158
  5.3 37.2 %collective-permute-start.2 = (s32[4,16]{1,0:T(4,128)S(1)}, s32[4,16]{1,0:T(4,128)S(1)}, u32[]{:S(2)}, u32[]{:S(2)}) collective-permute-start(s32[4,16]{1,0:T(4,128)S(1)} %pad_add_fusion), channel_id=1, source_target_pairs={{12,0},{16,4},{20,8},{24,12},{28,16},{0,20},{4,24},{8,28},{13,1},{... | collective-permute-start | bytes 776 | tf_op jit(solution)/shard_map/ppermute | solution.py:158
  6.7 32.1 %collective-permute-start = (s32[4,16]{1,0:T(4,128)S(1)}, s32[4,16]{1,0:T(4,128)S(1)}, u32[]{:S(2)}, u32[]{:S(2)}) collective-permute-start(s32[4,16]{1,0:T(4,128)S(1)} %pad_add_fusion), channel_id=1, source_target_pairs={{4,0},{8,4},{12,8},{16,12},{20,16},{24,20},{28,24},{0,28},{5,1},{9... | collective-permute-start | bytes 776 | tf_op jit(solution)/shard_map/ppermute | solution.py:158
  7.6 1.2 %copy-start = (bf16[8,16,4096]{2,1,0:T(8,128)(2,1)S(1)}, bf16[8,16,4096]{2,1,0:T(8,128)(2,1)}, u32[]{:S(2)}) copy-start(bf16[8,16,4096]{2,1,0:T(8,128)(2,1)} %values_ref.1) | copy-start | bytes 3145732
  8.8 1.0 copy-start.1
  33.7 5.0 %copy-start.2 = (s32[16]{0:T(128)S(1)}, s32[16]{0:T(128)}, u32[]{:S(2)}) copy-start(s32[16]{0:T(128)} %param.11) | copy-start | bytes 196
  33.7 5.0 %copy-start.3 = (s32[16]{0:T(128)S(1)}, s32[16]{0:T(128)}, u32[]{:S(2)}) copy-start(s32[16]{0:T(128)} %param.9) | copy-start | bytes 196
  33.7 5.0 %copy-start.4 = (s32[16]{0:T(128)S(1)}, s32[16]{0:T(128)}, u32[]{:S(2)}) copy-start(s32[16]{0:T(128)} %param.10) | copy-start | bytes 196
  33.7 5.0 %copy-start.5 = (s32[16,1]{0,1:T(1,128)S(1)}, s32[16,1]{0,1:T(1,128)}, u32[]{:S(2)}) copy-start(s32[16,1]{0,1:T(1,128)} %param.8) | copy-start | bytes 196
  33.7 30.8 %all-to-all-start = ((bf16[4,16,64,128]{3,2,1,0:T(8,128)(2,1)}), bf16[4,16,64,128]{3,2,1,0:T(8,128)(2,1)S(1)}, u32[]{:S(2)}, u32[]{:S(2)}) async-start(bf16[4,16,64,128]{3,2,1,0:T(8,128)(2,1)} %shard_map.64), calls=%async_computation | async-start | bytes 2097152 | tf_op jit(solution)/shard_map/all_to_all | solution.py:169
  38.8 3.6 %collective-permute-start.1 = (s32[4,16]{1,0:T(4,128)S(1)}, s32[4,16]{1,0:T(4,128)S(1)}, u32[]{:S(2)}, u32[]{:S(2)}) collective-permute-start(s32[4,16]{1,0:T(4,128)S(1)} %pad_add_fusion), channel_id=1, source_target_pairs={{8,0},{12,4},{16,8},{20,12},{24,16},{28,20},{0,24},{4,28},{9,1},{1... | collective-permute-start | bytes 776 | tf_op jit(solution)/shard_map/ppermute | solution.py:158
  42.4 3.9 %collective-permute-start.6 = (s32[4,16]{1,0:T(4,128)S(1)}, s32[4,16]{1,0:T(4,128)S(1)}, u32[]{:S(2)}, u32[]{:S(2)}) collective-permute-start(s32[4,16]{1,0:T(4,128)S(1)} %pad_add_fusion), channel_id=1, source_target_pairs={{28,0},{0,4},{4,8},{8,12},{12,16},{16,20},{20,24},{24,28},{29,1},{... | collective-permute-start | bytes 776 | tf_op jit(solution)/shard_map/ppermute | solution.py:158
  64.7 6.5 %collective-permute-start.7 = (bf16[16,64,128]{2,1,0:T(8,128)(2,1)S(1)}, bf16[16,64,128]{2,1,0:T(8,128)(2,1)S(1)}, u32[]{:S(2)}, u32[]{:S(2)}) collective-permute-start(bf16[16,64,128]{2,1,0:T(8,128)(2,1)S(1)} %reduce_sum.12), channel_id=1, source_target_pairs={{4,0},{8,4},{12,8},{16,12},{20,16},{24,20},{28,24},{0,28},{5,1},{9... | collective-permute-start | bytes 786440 | tf_op jit(solution)/shard_map/ppermute | solution.py:158
  64.9 30.2 %collective-permute-start.13 = (bf16[16,64,128]{2,1,0:T(8,128)(2,1)S(1)}, bf16[16,64,128]{2,1,0:T(8,128)(2,1)S(1)}, u32[]{:S(2)}, u32[]{:S(2)}) collective-permute-start(bf16[16,64,128]{2,1,0:T(8,128)(2,1)S(1)} %reduce_sum.12), channel_id=1, source_target_pairs={{28,0},{0,4},{4,8},{8,12},{12,16},{16,20},{20,24},{24,28},{29,1},{... | collective-permute-start | bytes 786440 | tf_op jit(solution)/shard_map/ppermute | solution.py:158
  65.4 29.6 %collective-permute-start.12 = (bf16[16,64,128]{2,1,0:T(8,128)(2,1)S(1)}, bf16[16,64,128]{2,1,0:T(8,128)(2,1)S(1)}, u32[]{:S(2)}, u32[]{:S(2)}) collective-permute-start(bf16[16,64,128]{2,1,0:T(8,128)(2,1)S(1)} %reduce_sum.12), channel_id=1, source_target_pairs={{24,0},{28,4},{0,8},{4,12},{8,16},{12,20},{16,24},{20,28},{25,1},{... | collective-permute-start | bytes 786440 | tf_op jit(solution)/shard_map/ppermute | solution.py:158
  65.7 29.3 %collective-permute-start.11 = (bf16[16,64,128]{2,1,0:T(8,128)(2,1)S(1)}, bf16[16,64,128]{2,1,0:T(8,128)(2,1)S(1)}, u32[]{:S(2)}, u32[]{:S(2)}) collective-permute-start(bf16[16,64,128]{2,1,0:T(8,128)(2,1)S(1)} %reduce_sum.12), channel_id=1, source_target_pairs={{20,0},{24,4},{28,8},{0,12},{4,16},{8,20},{12,24},{16,28},{21,1},{... | collective-permute-start | bytes 786440 | tf_op jit(solution)/shard_map/ppermute | solution.py:158
  67.6 21.0 %collective-permute-start.8 = (bf16[16,64,128]{2,1,0:T(8,128)(2,1)S(1)}, bf16[16,64,128]{2,1,0:T(8,128)(2,1)S(1)}, u32[]{:S(2)}, u32[]{:S(2)}) collective-permute-start(bf16[16,64,128]{2,1,0:T(8,128)(2,1)S(1)} %reduce_sum.12), channel_id=1, source_target_pairs={{8,0},{12,4},{16,8},{20,12},{24,16},{28,20},{0,24},{4,28},{9,1},{1... | collective-permute-start | bytes 786440 | tf_op jit(solution)/shard_map/ppermute | solution.py:158
  71.2 18.3 %collective-permute-start.9 = (bf16[16,64,128]{2,1,0:T(8,128)(2,1)S(1)}, bf16[16,64,128]{2,1,0:T(8,128)(2,1)S(1)}, u32[]{:S(2)}, u32[]{:S(2)}) collective-permute-start(bf16[16,64,128]{2,1,0:T(8,128)(2,1)S(1)} %reduce_sum.12), channel_id=1, source_target_pairs={{12,0},{16,4},{20,8},{24,12},{28,16},{0,20},{4,24},{8,28},{13,1},{... | collective-permute-start | bytes 786440 | tf_op jit(solution)/shard_map/ppermute | solution.py:158
  88.6 6.4 %collective-permute-start.10 = (bf16[16,64,128]{2,1,0:T(8,128)(2,1)S(1)}, bf16[16,64,128]{2,1,0:T(8,128)(2,1)S(1)}, u32[]{:S(2)}, u32[]{:S(2)}) collective-permute-start(bf16[16,64,128]{2,1,0:T(8,128)(2,1)S(1)} %reduce_sum.12), channel_id=1, source_target_pairs={{16,0},{20,4},{24,8},{28,12},{0,16},{4,20},{8,24},{12,28},{17,1},{... | collective-permute-start | bytes 786440 | tf_op jit(solution)/shard_map/ppermute | solution.py:158

commit v2 on v1

v2 whole, which is shorter than its diff:
```python
import functools

import jax
import jax.numpy as jnp
from jax import lax
from jax.experimental import pallas as pl
from jax.experimental.pallas import tpu as pltpu
from jax.sharding import PartitionSpec as P

W = 8
SUB = 64
TAPS = 8
TU = 128
NV = 2048
LANES = 128
SUBLANES = 8
BLOCKS = NV // LANES
META = 16
STEP = 4

VMEM = pl.BlockSpec(memory_space=pltpu.VMEM)
SMEM = pl.BlockSpec(memory_space=pltpu.SMEM)
ANY = pl.BlockSpec(memory_space=pl.ANY)


def taper(scaled):
    inner = jnp.maximum(0.0, 1.0 - scaled * scaled)
    return inner * inner


def grid_kernel(me_ref, values_ref, places_ref, *rest):
    parts_refs, values_wide, pair_sums = rest[:-2], rest[-2], rest[-1]
    comp_count, sub_count, row_count = values_ref.shape
    peers = len(parts_refs)
    kept = comp_count // peers * SUB
    for comp in range(comp_count):
        values_wide[comp * sub_count : (comp + 1) * sub_count, :] = values_ref[comp].astype(jnp.float32)
    cells = lax.broadcasted_iota(jnp.int32, (SUB, row_count), 0).astype(jnp.float32) * (2.0 / TAPS)

    def one_sub(sub):
        row_taps = taper(cells - places_ref[0, pl.ds(sub, 1), :] * (2.0 / TAPS)).astype(jnp.bfloat16)
        col_taps = taper(cells - places_ref[1, pl.ds(sub, 1), :] * (2.0 / TAPS))
        weighted = jnp.concatenate(
            [
                (values_wide[pl.ds(comp * sub_count + sub, 1), :] * col_taps).astype(jnp.bfloat16)
                for comp in range(comp_count)
            ],
            axis=0,
        )
        return lax.dot_general(
            weighted, row_taps, (((1,), (1,)), ((), ())), preferred_element_type=jnp.float32
        )

    def some_subs(turn, carry):
        for pair in range(STEP // 2):
            sub = turn * STEP + pair * 2
            pair_sums[pair] = jnp.concatenate([one_sub(sub), one_sub(sub + 1)], axis=1).astype(jnp.bfloat16)
        for pair in range(STEP // 2):
            for ahead, parts_ref in enumerate(parts_refs):
                peer = lax.rem(me_ref[0] + ahead, peers)
                rows = pl.ds(pl.multiple_of(peer * kept, kept), kept)
                parts_ref[turn * (STEP // 2) + pair] = pair_sums[pair, rows, :]
        return carry

    lax.fori_loop(0, sub_count // STEP, some_subs, 0)


def grid_parts(values, places, peers, chunk, sub_count):
    comp_count, _, row_count = values.shape
    kept = comp_count // peers * SUB
    me = lax.axis_index("tm").astype(jnp.int32).reshape(1)
    return pl.pallas_call(
        grid_kernel,
        grid=(1,),
        out_shape=[jax.ShapeDtypeStruct((sub_count // 2, kept, LANES), jnp.bfloat16)] * peers,
        in_specs=[
            SMEM,
            pl.BlockSpec((comp_count, sub_count, row_count), lambda i: (0, chunk, 0)),
            pl.BlockSpec((2, sub_count, row_count), lambda i: (0, chunk, 0)),
        ],
        out_specs=[pl.BlockSpec((sub_count // 2, kept, LANES), lambda i: (0, 0, 0))] * peers,
        scratch_shapes=[
            pltpu.VMEM((comp_count * sub_count, row_count), jnp.float32),
            pltpu.VMEM((STEP // 2, comp_count * SUB, LANES), jnp.bfloat16),
        ],
        compiler_params=pltpu.CompilerParams(vmem_limit_bytes=48 << 20),
        cost_estimate=pl.CostEstimate(
            flops=8 * sub_count * row_count * SUB * SUB * comp_count,
            bytes_accessed=2 << 20,
            transcendentals=0,
        ),
    )(me, values, places)


def sum_kernel(*refs):
    numbers_ref, parts_refs, out_ref = refs[0], refs[1:-1], refs[-1]
    pairs = parts_refs[0].shape[0]
    for pair in range(pairs):
        total = parts_refs[0][pair].astype(jnp.float32)
        for parts_ref in parts_refs[1:]:
            total = total + parts_ref[pair].astype(jnp.float32)
        out_ref[pair * 2 * SUB : (pair + 1) * 2 * SUB, :] = total.T.astype(jnp.bfloat16)
    out_ref[pairs * 2 * SUB :, :] = numbers_ref[...].astype(jnp.bfloat16)


def sum_parts(parts, numbers):
    pairs, kept, _ = parts[0].shape
    return pl.pallas_call(
        sum_kernel,
        out_shape=jax.ShapeDtypeStruct((pairs * 2 * SUB + META, kept), jnp.bfloat16),
        in_specs=[VMEM] * (1 + len(parts)),
        out_specs=VMEM,
        compiler_params=pltpu.CompilerParams(vmem_limit_bytes=8 << 20),
        cost_estimate=pl.CostEstimate(flops=1 << 20, bytes_accessed=2 << 20, transcendentals=0),
    )(numbers, *parts)


def exchange(parts, axis):
    size = lax.axis_size(axis)
    return [parts[0]] + [
        lax.ppermute(parts[by], axis, [(i, (i + by) % size) for i in range(size)]) for by in range(1, size)
    ]


def gather_all(array, axis):
    size = lax.axis_size(axis)
    near = [array] + [
        lax.ppermute(array, axis, [(i, i ^ mask) for i in range(size)]) for mask in range(2, size, 2)
    ]
    near = jnp.stack(near, axis=0)
    other = lax.ppermute(near, axis, [(i, i ^ 1) for i in range(size)])
    return [near, other]


def zero_kernel(token_ref, out_ref, blank, sem):
    blank[...] = jnp.zeros(blank.shape, jnp.float32)
    copies = [pltpu.make_async_copy(blank, out_ref.at[:, plane], sem.at[plane]) for plane in range(W)]
    for copy in copies:
        copy.start()
    for copy in copies:
        copy.wait()


def blank_tile(token, comp_count):
    return pl.pallas_call(
        zero_kernel,
        out_shape=jax.ShapeDtypeStruct((comp_count, W, TU, NV), jnp.float32),
        in_specs=[ANY],
        out_specs=ANY,
        scratch_shapes=[pltpu.VMEM((comp_count, TU, NV), jnp.float32), pltpu.SemaphoreType.DMA((W,))],
        compiler_params=pltpu.CompilerParams(vmem_limit_bytes=8 << 20),
        cost_estimate=pl.CostEstimate(
            flops=0, bytes_accessed=comp_count * W * TU * NV * 4, transcendentals=0
        ),
    )(token)


def plan_kernel(placing_ref, count_ref, listed_ref, used_count_ref, used_ref, touched):
    sources, _, per_source = placing_ref.shape

    def clear(index, carry):
        touched[index] = 0
        return carry

    lax.fori_loop(0, W * BLOCKS, clear, 0)
    for plane in range(W):
        used_count_ref[plane] = 0
        for source in range(sources):
            count_ref[source, plane] = 0
    for source in range(sources):

        def enlist(sub, carry, source=source):
            @pl.when(placing_ref[source, 0, sub] >= 0)
            def _():
                plane = placing_ref[source, 1, sub]
                col = placing_ref[source, 2, sub]
                at = count_ref[source, plane]
                listed_ref[source, plane, at] = sub
                count_ref[source, plane] = at + 1

                def use(block):
                    @pl.when(touched[plane * BLOCKS + block] == 0)
                    def _():
                        touched[plane * BLOCKS + block] = 1
                        used_at = used_count_ref[plane]
                        used_ref[plane, used_at] = block
                        used_count_ref[plane] = used_at + 1

                use(col // LANES)

                @pl.when(col % LANES > LANES - SUB)
                def _():
                    use(col // LANES + 1)

            return carry

        lax.fori_loop(0, per_source, enlist, 0)


def plan(placing):
    sources, _, per_source = placing.shape
    return pl.pallas_call(
        plan_kernel,
        out_shape=[
            jax.ShapeDtypeStruct((sources, W), jnp.int32),
            jax.ShapeDtypeStruct((sources, W, per_source), jnp.int32),
            jax.ShapeDtypeStruct((W,), jnp.int32),
            jax.ShapeDtypeStruct((W, BLOCKS), jnp.int32),
        ],
        in_specs=[SMEM],
        out_specs=[SMEM] * 4,
        scratch_shapes=[pltpu.SMEM((W * BLOCKS,), jnp.int32)],
        cost_estimate=pl.CostEstimate(flops=0, bytes_accessed=4 << 20, transcendentals=0),
    )(placing)


def place_kernel(placing_ref, count_ref, listed_ref, used_count_ref, used_ref, *rest):
    sources = count_ref.shape[0]
    arrays, out_ref, canvas, sem = rest[:sources], rest[sources + 1], rest[-2], rest[-1]
    comp_count = canvas.shape[1]
    per_array = listed_ref.shape[2] // arrays[0].shape[0]
    lane = lax.broadcasted_iota(jnp.int32, (SUB + SUBLANES, LANES), 1)

    def lanes_of(block):
        return pl.ds(pl.multiple_of(block * LANES, LANES), LANES)

    def out_copy(plane, block):
        return pltpu.make_async_copy(
            canvas.at[plane, :, pl.ds(SUB, TU), lanes_of(block)],
            out_ref.at[:, plane, :, lanes_of(block)],
            sem.at[plane, block],
        )

    def add_patch(source, plane, index):
        sub = listed_ref[source, plane, index]
        start = placing_ref[source, 0, sub]
        col = placing_ref[source, 2, sub]
        block = col // LANES
        shift = col % LANES
        at = pl.ds(pl.multiple_of(sub % per_array * SUB, SUB), SUB)
        patch = arrays[source][sub // per_array, at, :].astype(jnp.float32)
        if patch.shape[1] < LANES:
            patch = jnp.concatenate([patch] * (LANES // patch.shape[1]), axis=1)
        patch = jnp.concatenate([patch, jnp.zeros((SUBLANES, patch.shape[1]), jnp.float32)], axis=0)
        patch = pltpu.roll(patch, start % SUBLANES, 0)
        rows = pl.ds(pl.multiple_of(start // SUBLANES * SUBLANES, SUBLANES), SUB + SUBLANES)
        for comp in range(comp_count):
            turned = patch[:, comp // 2 * LANES : (comp // 2 + 1) * LANES]
            turned = pltpu.roll(turned, (shift + comp % 2 * SUB) % LANES, 1)
            here = (lane >= shift) & (lane < shift + SUB)
            canvas[plane, comp, rows, lanes_of(block)] += jnp.where(here, turned, 0.0)

            @pl.when(shift > LANES - SUB)
            def _():
                canvas[plane, comp, rows, lanes_of(block + 1)] += jnp.where(
                    lane < shift + SUB - LANES, turned, 0.0
                )

    for plane in range(W):

        def clear(index, carry, plane=plane):
            block = used_ref[plane, index]
            canvas[plane, :, pl.ds(SUB, TU), lanes_of(block)] = jnp.zeros((comp_count, TU, LANES), jnp.float32)
            return carry

        lax.fori_loop(0, used_count_ref[plane], clear, 0)
        for source in range(sources):

            def add(index, carry, plane=plane, source=source):
                add_patch(source, plane, index)
                return carry

            lax.fori_loop(0, count_ref[source, plane], add, 0)

        def send(index, carry, plane=plane):
            out_copy(plane, used_ref[plane, index]).start()
            return carry

        lax.fori_loop(0, used_count_ref[plane], send, 0)
    for plane in range(W):

        def finish(index, carry, plane=plane):
            out_copy(plane, used_ref[plane, index]).wait()
            return carry

        lax.fori_loop(0, used_count_ref[plane], finish, 0)


def place_all(arrays, placing, plans, tile_grid):
    comp_count = tile_grid.shape[0]
    return pl.pallas_call(
        place_kernel,
        out_shape=jax.ShapeDtypeStruct(tile_grid.shape, jnp.float32),
        in_specs=[SMEM] * 5 + [VMEM] * len(arrays) + [ANY],
        out_specs=ANY,
        scratch_shapes=[
            pltpu.VMEM((W, comp_count, TU + 2 * SUB, NV), jnp.float32),
            pltpu.SemaphoreType.DMA((W, BLOCKS)),
        ],
        input_output_aliases={5 + len(arrays): 0},
        compiler_params=pltpu.CompilerParams(vmem_limit_bytes=44 << 20),
        cost_estimate=pl.CostEstimate(flops=0, bytes_accessed=16 << 20, transcendentals=0),
    )(placing, *plans, *arrays, tile_grid)


def body(visibilities, positions, owner, w_plane, row_offset, col_offset):
    peers = lax.axis_size("tm")
    tiles = lax.axis_size("uv")
    sub_count = visibilities.shape[1]
    comp_count = visibilities.shape[0] // peers
    kept = comp_count * SUB
    tile = lax.axis_index("uv")
    half = sub_count // 2

    numbers = jnp.stack(
        [owner[:, 0], row_offset, w_plane, col_offset // LANES, col_offset % LANES], axis=0
    ).astype(jnp.float32)
    numbers = jnp.pad(numbers, ((0, META - 5), (0, kept - sub_count)))

    sent_a = grid_parts(visibilities, positions, peers, 0, half)
    parts_a = exchange(sent_a, "tm")
    sent_b = grid_parts(visibilities, positions, peers, 1, half)
    parts_b = exchange(sent_b, "tm")
    arrays_a = gather_all(sum_parts(parts_a, numbers), "uv")
    tile_grid = blank_tile(sent_b[0], comp_count)

    told = jnp.stack(arrays_a, axis=0)[:, :, half * SUB :, :sub_count].astype(jnp.float32).astype(jnp.int32)
    told = jnp.transpose(told, (2, 0, 1, 3))
    ahead = (told[0] - tile) % tiles
    starts = jnp.where(ahead == 0, told[1] + SUB, jnp.where(ahead == tiles - 1, told[1] + SUB - TU, -1))
    placing = jnp.stack([starts, told[2], told[3] * LANES + told[4]], axis=0)
    placing = jnp.transpose(placing, (1, 0, 2, 3))
    placing = jnp.concatenate(
        [
            placing[:, :, :, :half].reshape(2, 3, -1),
            placing[:, :, :, half:].reshape(2, 3, -1),
        ],
        axis=0,
    )
    plans = plan(placing)
    arrays_b = gather_all(sum_parts(parts_b, numbers), "uv")
    return place_all(arrays_a + arrays_b, placing, plans, tile_grid)


def solution(mesh):
    placed = (P(None, "uv", "tm"), P(None, "uv", "tm"), P("uv", None), P("uv"), P("uv"), P("uv"))
    return jax.shard_map(
        body, mesh=mesh, in_specs=placed, out_specs=P("tm", None, "uv", None), check_vma=False
    )
```

time: 110 us -> 94 us (0.85)
  the two profiles are of different devices: /device:TPU:0 before, /device:TPU:10 now
where the time goes in v2:
time: 94 us; the launch traced here: 93.4 us
  Pallas kernels  45.2 us (48%)
  waiting for transfers between devices  26.4 us (28%)
  starting transfers between devices  14.6 us (16%)
  local copies, waits for them, and re-layouts  6.57 us (7%)
    ppermute x6, waiting for transfers between devices, exchange(): lax.ppermute(parts[by], axis, [(i, (i + by) % size) for i in range(size)])  20.5 us
    pallas_call x2, Pallas kernels, grid_parts(): pl.pallas_call(grid_kernel, grid=(1,), out_shape=[jax.ShapeDtypeStruct((s...  19.3 us
    pallas_call x1, Pallas kernels, place_all(): pl.pallas_call(place_kernel, out_shape=jax.ShapeDtypeStruct(tile_grid.sha...  11.1 us
    pallas_call x1, Pallas kernels, plan(): pl.pallas_call(plan_kernel, out_shape=[jax.ShapeDtypeStruct((sources, W),...  8.45 us
    ppermute x6, starting transfers between devices, exchange(): lax.ppermute(parts[by], axis, [(i, (i + by) % size) for i in range(size)])  7.32 us
    ppermute x6, starting transfers between devices, gather_all(): lax.ppermute(array, axis, [(i, i ^ mask) for i in range(size)])  7.11 us
    unnamed x29, local copies, waits for them, and re-layouts  6.27 us
    pallas_call x1, Pallas kernels, blank_tile(): pl.pallas_call(zero_kernel, out_shape=jax.ShapeDtypeStruct((comp_count, W...  6.06 us
  transfers between devices with their start and end apart: 14, of which 9 were waited for; matrix products, arithmetic and copies ran while one was open for 0% of the time, Pallas kernels for 26%

profile of v2, /device:TPU:10, one launch (start us, length us, event | category | flops | bytes accessed | tf_op | source)
XLA Modules:
  0.0 93.4 jit_solution(14199555077948942491)
XLA Ops:
  0.0 1.3 %copy-done.6 = bf16[8,16,4096]{2,1,0:T(8,128)(2,1)S(1)} copy-done((bf16[8,16,4096]{2,1,0:T(8,128)(2,1)S(1)}, bf16[8,16,4096]{2,1,0:T(8,128)(2,1)}, u32[]{:S(2)}) %copy-start.6) | copy-done | bytes 1048600
  1.3 1.0 %copy-done.8 = f32[2,16,4096]{2,1,0:T(8,128)S(1)} copy-done((f32[2,16,4096]{2,1,0:T(8,128)S(1)}, f32[2,16,4096]{2,1,0:T(8,128)}, u32[]{:S(2)}) %copy-start.8) | copy-done | bytes 524312
  2.3 9.6 %shard_map.64 = (bf16[4,128,128]{2,1,0:T(8,128)(2,1)S(1)}, bf16[4,128,128]{2,1,0:T(8,128)(2,1)S(1)}, bf16[4,128,128]{2,1,0:T(8,128)(2,1)S(1)}, bf16[4,128,128]{2,1,0:T(8,128)(2,1)S(1)}) custom-call(s32[1]{0:T(128)} %bitcast.5.me_ref, bf16[8,16,4096]{2,1,0:T(8,128)(2,1)S(1)} %copy-done.6, f32[2,16,4096]{2,1,0:T(8,128)S(1)} %copy-done.8), custom_call_target="tpu_custom_call" | custom-call | flops 8589934592 | bytes 2097152 | tf_op jit(solution)/shard_map/pallas_call | solution.py:72
  12.0 1.6 %collective-permute-start = (bf16[4,128,128]{2,1,0:T(8,128)(2,1)S(1)}, bf16[4,128,128]{2,1,0:T(8,128)(2,1)S(1)}, u32[]{:S(2)}, u32[]{:S(2)}) collective-permute-start(bf16[4,128,128]{2,1,0:T(8,128)(2,1)S(1)} %get-tuple-element.18), channel_id=1, source_target_pairs={{0,1},{1,2},{2,3},{3,0},{4,5},{5,6},{6,7},{7,4},{8,9},{9,10},{10,1... | collective-permute-start | bytes 393224 | tf_op jit(solution)/shard_map/ppermute | solution.py:121
  13.6 1.2 %collective-permute-start.1 = (bf16[4,128,128]{2,1,0:T(8,128)(2,1)S(1)}, bf16[4,128,128]{2,1,0:T(8,128)(2,1)S(1)}, u32[]{:S(2)}, u32[]{:S(2)}) collective-permute-start(bf16[4,128,128]{2,1,0:T(8,128)(2,1)S(1)} %get-tuple-element.19), channel_id=1, source_target_pairs={{0,2},{1,3},{2,0},{3,1},{4,6},{5,7},{6,4},{7,5},{8,10},{9,11},{10,... | collective-permute-start | bytes 393224 | tf_op jit(solution)/shard_map/ppermute | solution.py:121
  14.8 1.8 %collective-permute-start.2 = (bf16[4,128,128]{2,1,0:T(8,128)(2,1)S(1)}, bf16[4,128,128]{2,1,0:T(8,128)(2,1)S(1)}, u32[]{:S(2)}, u32[]{:S(2)}) collective-permute-start(bf16[4,128,128]{2,1,0:T(8,128)(2,1)S(1)} %get-tuple-element.20), channel_id=1, source_target_pairs={{0,3},{1,0},{2,1},{3,2},{4,7},{5,4},{6,5},{7,6},{8,11},{9,8},{10,9... | collective-permute-start | bytes 393224 | tf_op jit(solution)/shard_map/ppermute | solution.py:121
  16.7 6.4 %collective-permute-done.refs_2_ = bf16[4,128,128]{2,1,0:T(8,128)(2,1)S(1)} collective-permute-done((bf16[4,128,128]{2,1,0:T(8,128)(2,1)S(1)}, bf16[4,128,128]{2,1,0:T(8,128)(2,1)S(1)}, u32[]{:S(2)}, u32[]{:S(2)}) %collective-permute-start) | collective-permute-done | bytes 131104 | tf_op jit(solution)/shard_map/ppermute | solution.py:121
  23.1 1.7 %collective-permute-done.1.refs_3_ = bf16[4,128,128]{2,1,0:T(8,128)(2,1)S(1)} collective-permute-done((bf16[4,128,128]{2,1,0:T(8,128)(2,1)S(1)}, bf16[4,128,128]{2,1,0:T(8,128)(2,1)S(1)}, u32[]{:S(2)}, u32[]{:S(2)}) %collective-permute-start.1) | collective-permute-done | bytes 131104 | tf_op jit(solution)/shard_map/ppermute | solution.py:121
  24.8 1.8 %collective-permute-done.2.refs_4_ = bf16[4,128,128]{2,1,0:T(8,128)(2,1)S(1)} collective-permute-done((bf16[4,128,128]{2,1,0:T(8,128)(2,1)S(1)}, bf16[4,128,128]{2,1,0:T(8,128)(2,1)S(1)}, u32[]{:S(2)}, u32[]{:S(2)}) %collective-permute-start.2) | collective-permute-done | bytes 131104 | tf_op jit(solution)/shard_map/ppermute | solution.py:121
  26.7 1.6 %collective-permute-start.5 = (bf16[528,128]{1,0:T(8,128)(2,1)S(1)}, bf16[528,128]{1,0:T(8,128)(2,1)S(1)}, u32[]{:S(2)}, u32[]{:S(2)}) collective-permute-start(bf16[528,128]{1,0:T(8,128)(2,1)S(1)} %shard_map.65), channel_id=1, source_target_pairs={{0,24},{4,28},{8,16},{12,20},{16,8},{20,12},{24,0},{28,4},{1,25},{... | collective-permute-start | bytes 405512 | tf_op jit(solution)/shard_map/ppermute | solution.py:128
  28.7 1.5 %collective-permute-start.3 = (bf16[528,128]{1,0:T(8,128)(2,1)S(1)}, bf16[528,128]{1,0:T(8,128)(2,1)S(1)}, u32[]{:S(2)}, u32[]{:S(2)}) collective-permute-start(bf16[528,128]{1,0:T(8,128)(2,1)S(1)} %shard_map.65), channel_id=1, source_target_pairs={{0,8},{4,12},{8,0},{12,4},{16,24},{20,28},{24,16},{28,20},{1,9},{5... | collective-permute-start | bytes 405512 | tf_op jit(solution)/shard_map/ppermute | solution.py:128
  30.2 3.9 %collective-permute-done.5 = bf16[528,128]{1,0:T(8,128)(2,1)S(1)} collective-permute-done((bf16[528,128]{1,0:T(8,128)(2,1)S(1)}, bf16[528,128]{1,0:T(8,128)(2,1)S(1)}, u32[]{:S(2)}, u32[]{:S(2)}) %collective-permute-start.5) | collective-permute-done | bytes 135200 | tf_op jit(solution)/shard_map/ppermute | solution.py:128
  34.1 1.9 %collective-permute-done.4 = bf16[528,128]{1,0:T(8,128)(2,1)S(1)} collective-permute-done((bf16[528,128]{1,0:T(8,128)(2,1)S(1)}, bf16[528,128]{1,0:T(8,128)(2,1)S(1)}, u32[]{:S(2)}, u32[]{:S(2)}) %collective-permute-start.4) | collective-permute-done | bytes 135200 | tf_op jit(solution)/shard_map/ppermute | solution.py:128
  36.3 9.6 %shard_map.67 = (bf16[4,128,128]{2,1,0:T(8,128)(2,1)S(1)}, bf16[4,128,128]{2,1,0:T(8,128)(2,1)S(1)}, bf16[4,128,128]{2,1,0:T(8,128)(2,1)S(1)}, bf16[4,128,128]{2,1,0:T(8,128)(2,1)S(1)}) custom-call(s32[1]{0:T(128)} %bitcast.5.me_ref, bf16[8,16,4096]{2,1,0:T(8,128)(2,1)S(1)} %copy-done.7, f32[2,16,4096]{2,1,0:T(8,128)S(1)} %copy-done.9), custom_call_target="tpu_custom_call" | custom-call | flops 8589934592 | bytes 2097152 | tf_op jit(solution)/shard_map/pallas_call | solution.py:72
  46.1 1.0 %collective-permute-start.8 = (bf16[4,128,128]{2,1,0:T(8,128)(2,1)S(1)}, bf16[4,128,128]{2,1,0:T(8,128)(2,1)S(1)}, u32[]{:S(2)}, u32[]{:S(2)}) collective-permute-start(bf16[4,128,128]{2,1,0:T(8,128)(2,1)S(1)} %get-tuple-element.27), channel_id=1, source_target_pairs={{0,2},{1,3},{2,0},{3,1},{4,6},{5,7},{6,4},{7,5},{8,10},{9,11},{10,... | collective-permute-start | bytes 393224 | tf_op jit(solution)/shard_map/ppermute | solution.py:121
  47.1 1.6 %collective-permute-start.9 = (bf16[4,128,128]{2,1,0:T(8,128)(2,1)S(1)}, bf16[4,128,128]{2,1,0:T(8,128)(2,1)S(1)}, u32[]{:S(2)}, u32[]{:S(2)}) collective-permute-start(bf16[4,128,128]{2,1,0:T(8,128)(2,1)S(1)} %get-tuple-element.28), channel_id=1, source_target_pairs={{0,3},{1,0},{2,1},{3,2},{4,7},{5,4},{6,5},{7,6},{8,11},{9,8},{10,9... | collective-permute-start | bytes 393224 | tf_op jit(solution)/shard_map/ppermute | solution.py:121
  48.6 3.7 %collective-permute-done.7.refs_2_ = bf16[4,128,128]{2,1,0:T(8,128)(2,1)S(1)} collective-permute-done((bf16[4,128,128]{2,1,0:T(8,128)(2,1)S(1)}, bf16[4,128,128]{2,1,0:T(8,128)(2,1)S(1)}, u32[]{:S(2)}, u32[]{:S(2)}) %collective-permute-start.7) | collective-permute-done | bytes 131104 | tf_op jit(solution)/shard_map/ppermute | solution.py:121
  52.3 5.8 %collective-permute-done.8.refs_3_ = bf16[4,128,128]{2,1,0:T(8,128)(2,1)S(1)} collective-permute-done((bf16[4,128,128]{2,1,0:T(8,128)(2,1)S(1)}, bf16[4,128,128]{2,1,0:T(8,128)(2,1)S(1)}, u32[]{:S(2)}, u32[]{:S(2)}) %collective-permute-start.8) | collective-permute-done | bytes 131104 | tf_op jit(solution)/shard_map/ppermute | solution.py:121
  58.2 1.2 %collective-permute-done.9.refs_4_ = bf16[4,128,128]{2,1,0:T(8,128)(2,1)S(1)} collective-permute-done((bf16[4,128,128]{2,1,0:T(8,128)(2,1)S(1)}, bf16[4,128,128]{2,1,0:T(8,128)(2,1)S(1)}, u32[]{:S(2)}, u32[]{:S(2)}) %collective-permute-start.9) | collective-permute-done | bytes 131104 | tf_op jit(solution)/shard_map/ppermute | solution.py:121
  59.5 1.5 %collective-permute-start.12 = (bf16[528,128]{1,0:T(8,128)(2,1)S(1)}, bf16[528,128]{1,0:T(8,128)(2,1)S(1)}, u32[]{:S(2)}, u32[]{:S(2)}) collective-permute-start(bf16[528,128]{1,0:T(8,128)(2,1)S(1)} %shard_map.68), channel_id=1, source_target_pairs={{0,24},{4,28},{8,16},{12,20},{16,8},{20,12},{24,0},{28,4},{1,25},{... | collective-permute-start | bytes 405512 | tf_op jit(solution)/shard_map/ppermute | solution.py:128
  61.5 1.5 %collective-permute-start.10 = (bf16[528,128]{1,0:T(8,128)(2,1)S(1)}, bf16[528,128]{1,0:T(8,128)(2,1)S(1)}, u32[]{:S(2)}, u32[]{:S(2)}) collective-permute-start(bf16[528,128]{1,0:T(8,128)(2,1)S(1)} %shard_map.68), channel_id=1, source_target_pairs={{0,8},{4,12},{8,0},{12,4},{16,24},{20,28},{24,16},{28,20},{1,9},{5... | collective-permute-start | bytes 405512 | tf_op jit(solution)/shard_map/ppermute | solution.py:128
  63.0 6.1 %shard_map.69.rest_4_ = f32[2,8,128,2048]{3,2,1,0:T(8,128)} custom-call(bf16[4,128,128]{2,1,0:T(8,128)(2,1)S(1)} %get-tuple-element.25.refs_1_.token_ref), custom_call_target="tpu_custom_call" | custom-call | bytes 16777216 | tf_op jit(solution)/shard_map/pallas_call | solution.py:145
  70.3 8.4 %shard_map.66 = (s32[4,8]{1,0:T(4,128)}, s32[4,8,32]{2,1,0:T(8,128)}, s32[8]{0:T(128)}, s32[8,16]{1,0:T(8,128)}) custom-call(s32[4,3,32]{2,1,0:T(4,128)} %copy-done), custom_call_target="tpu_custom_call" | custom-call | bytes 4194304 | tf_op jit(solution)/shard_map/pallas_call | solution.py:202
  82.1 11.1 %shard_map.70 = f32[2,8,128,2048]{3,2,1,0:T(8,128)} custom-call(s32[4,3,32]{2,1,0:T(4,128)S(1)} %copy-done.1, s32[4,8]{1,0:T(4,128)S(1)} %copy-done.4, s32[4,8,32]{2,1,0:T(8,128)S(1)} %copy-done.2, s32[8]{0:T(128)S(1)} %copy-done.5, s32[8,16]{1,0:T(8,128)S(1)} %copy-done.3, ...), custom_call_target="tpu_custom_call", output_to_operand_aliasing={{}: (9, {})} | custom-call | bytes 16777216 | tf_op jit(solution)/shard_map/pallas_call | solution.py:291
  (55 shorter events, 6.2 us)
Async XLA Ops:
  0.0 16.6 %copy-start.13 = (s32[16]{0:T(128)S(1)}, s32[16]{0:T(128)}, u32[]{:S(2)}) copy-start(s32[16]{0:T(128)} %param.11) | copy-start | bytes 196
  0.0 16.7 %copy-start.11 = (s32[16]{0:T(128)S(1)}, s32[16]{0:T(128)}, u32[]{:S(2)}) copy-start(s32[16]{0:T(128)} %param.10) | copy-start | bytes 196
  0.0 16.7 %copy-start.12 = (s32[16]{0:T(128)S(1)}, s32[16]{0:T(128)}, u32[]{:S(2)}) copy-start(s32[16]{0:T(128)} %param.9) | copy-start | bytes 196
  0.0 16.7 %copy-start.10 = (s32[16,1]{0,1:T(1,128)S(1)}, s32[16,1]{0,1:T(1,128)}, u32[]{:S(2)}) copy-start(s32[16,1]{0,1:T(1,128)} %param.8) | copy-start | bytes 196
  0.0 1.3 %copy-start.6 = (bf16[8,16,4096]{2,1,0:T(8,128)(2,1)S(1)}, bf16[8,16,4096]{2,1,0:T(8,128)(2,1)}, u32[]{:S(2)}) copy-start(bf16[8,16,4096]{2,1,0:T(8,128)(2,1)} %values_ref.3) | copy-start | bytes 3145732
  1.3 1.0 %copy-start.8 = (f32[2,16,4096]{2,1,0:T(8,128)S(1)}, f32[2,16,4096]{2,1,0:T(8,128)}, u32[]{:S(2)}) copy-start(f32[2,16,4096]{2,1,0:T(8,128)} %places_ref.3) | copy-start | bytes 1572868
  2.3 34.0 %copy-start.7 = (bf16[8,16,4096]{2,1,0:T(8,128)(2,1)S(1)}, bf16[8,16,4096]{2,1,0:T(8,128)(2,1)}, u32[]{:S(2)}) copy-start(bf16[8,16,4096]{2,1,0:T(8,128)(2,1)} %values_ref.3) | copy-start | bytes 3145732
  2.3 34.0 %copy-start.9 = (f32[2,16,4096]{2,1,0:T(8,128)S(1)}, f32[2,16,4096]{2,1,0:T(8,128)}, u32[]{:S(2)}) copy-start(f32[2,16,4096]{2,1,0:T(8,128)} %places_ref.3) | copy-start | bytes 1572868
  12.0 11.2 %collective-permute-start = (bf16[4,128,128]{2,1,0:T(8,128)(2,1)S(1)}, bf16[4,128,128]{2,1,0:T(8,128)(2,1)S(1)}, u32[]{:S(2)}, u32[]{:S(2)}) collective-permute-start(bf16[4,128,128]{2,1,0:T(8,128)(2,1)S(1)} %get-tuple-element.18), channel_id=1, source_target_pairs={{0,1},{1,2},{2,3},{3,0},{4,5},{5,6},{6,7},{7,4},{8,9},{9,10},{10,1... | collective-permute-start | bytes 393224 | tf_op jit(solution)/shard_map/ppermute | solution.py:121
  13.6 11.2 %collective-permute-start.1 = (bf16[4,128,128]{2,1,0:T(8,128)(2,1)S(1)}, bf16[4,128,128]{2,1,0:T(8,128)(2,1)S(1)}, u32[]{:S(2)}, u32[]{:S(2)}) collective-permute-start(bf16[4,128,128]{2,1,0:T(8,128)(2,1)S(1)} %get-tuple-element.19), channel_id=1, source_target_pairs={{0,2},{1,3},{2,0},{3,1},{4,6},{5,7},{6,4},{7,5},{8,10},{9,11},{10,... | collective-permute-start | bytes 393224 | tf_op jit(solution)/shard_map/ppermute | solution.py:121
  14.8 11.7 %collective-permute-start.2 = (bf16[4,128,128]{2,1,0:T(8,128)(2,1)S(1)}, bf16[4,128,128]{2,1,0:T(8,128)(2,1)S(1)}, u32[]{:S(2)}, u32[]{:S(2)}) collective-permute-start(bf16[4,128,128]{2,1,0:T(8,128)(2,1)S(1)} %get-tuple-element.20), channel_id=1, source_target_pairs={{0,3},{1,0},{2,1},{3,2},{4,7},{5,4},{6,5},{7,6},{8,11},{9,8},{10,9... | collective-permute-start | bytes 393224 | tf_op jit(solution)/shard_map/ppermute | solution.py:121
  26.7 7.4 %collective-permute-start.5 = (bf16[528,128]{1,0:T(8,128)(2,1)S(1)}, bf16[528,128]{1,0:T(8,128)(2,1)S(1)}, u32[]{:S(2)}, u32[]{:S(2)}) collective-permute-start(bf16[528,128]{1,0:T(8,128)(2,1)S(1)} %shard_map.65), channel_id=1, source_target_pairs={{0,24},{4,28},{8,16},{12,20},{16,8},{20,12},{24,0},{28,4},{1,25},{... | collective-permute-start | bytes 405512 | tf_op jit(solution)/shard_map/ppermute | solution.py:128
  28.2 7.8 %collective-permute-start.4 = (bf16[528,128]{1,0:T(8,128)(2,1)S(1)}, bf16[528,128]{1,0:T(8,128)(2,1)S(1)}, u32[]{:S(2)}, u32[]{:S(2)}) collective-permute-start(bf16[528,128]{1,0:T(8,128)(2,1)S(1)} %shard_map.65), channel_id=1, source_target_pairs={{0,16},{4,20},{8,24},{12,28},{16,0},{20,4},{24,8},{28,12},{1,17},{... | collective-permute-start | bytes 405512 | tf_op jit(solution)/shard_map/ppermute | solution.py:128
  28.7 7.4 %collective-permute-start.3 = (bf16[528,128]{1,0:T(8,128)(2,1)S(1)}, bf16[528,128]{1,0:T(8,128)(2,1)S(1)}, u32[]{:S(2)}, u32[]{:S(2)}) collective-permute-start(bf16[528,128]{1,0:T(8,128)(2,1)S(1)} %shard_map.65), channel_id=1, source_target_pairs={{0,8},{4,12},{8,0},{12,4},{16,24},{20,28},{24,16},{28,20},{1,9},{5... | collective-permute-start | bytes 405512 | tf_op jit(solution)/shard_map/ppermute | solution.py:128
  36.2 33.0 %collective-permute-start.6 = (bf16[4,528,128]{2,1,0:T(8,128)(2,1)S(1)}, bf16[4,528,128]{2,1,0:T(8,128)(2,1)S(1)}, u32[]{:S(2)}, u32[]{:S(2)}) collective-permute-start(bf16[4,528,128]{2,1,0:T(8,128)(2,1)S(1)} %get-tuple-element.30.rest_0_), channel_id=1, source_target_pairs={{0,4},{4,0},{8,12},{12,8},{16,20},{20,16},{24,28},{28,24},{1,5},{5... | collective-permute-start | bytes 1622024 | tf_op jit(solution)/shard_map/ppermute | solution.py:131
  46.0 6.4 %collective-permute-start.7 = (bf16[4,128,128]{2,1,0:T(8,128)(2,1)S(1)}, bf16[4,128,128]{2,1,0:T(8,128)(2,1)S(1)}, u32[]{:S(2)}, u32[]{:S(2)}) collective-permute-start(bf16[4,128,128]{2,1,0:T(8,128)(2,1)S(1)} %get-tuple-element.26), channel_id=1, source_target_pairs={{0,1},{1,2},{2,3},{3,0},{4,5},{5,6},{6,7},{7,4},{8,9},{9,10},{10,1... | collective-permute-start | bytes 393224 | tf_op jit(solution)/shard_map/ppermute | solution.py:121
  46.1 12.1 %collective-permute-start.8 = (bf16[4,128,128]{2,1,0:T(8,128)(2,1)S(1)}, bf16[4,128,128]{2,1,0:T(8,128)(2,1)S(1)}, u32[]{:S(2)}, u32[]{:S(2)}) collective-permute-start(bf16[4,128,128]{2,1,0:T(8,128)(2,1)S(1)} %get-tuple-element.27), channel_id=1, source_target_pairs={{0,2},{1,3},{2,0},{3,1},{4,6},{5,7},{6,4},{7,5},{8,10},{9,11},{10,... | collective-permute-start | bytes 393224 | tf_op jit(solution)/shard_map/ppermute | solution.py:121
  47.1 12.3 %collective-permute-start.9 = (bf16[4,128,128]{2,1,0:T(8,128)(2,1)S(1)}, bf16[4,128,128]{2,1,0:T(8,128)(2,1)S(1)}, u32[]{:S(2)}, u32[]{:S(2)}) collective-permute-start(bf16[4,128,128]{2,1,0:T(8,128)(2,1)S(1)} %get-tuple-element.28), channel_id=1, source_target_pairs={{0,3},{1,0},{2,1},{3,2},{4,7},{5,4},{6,5},{7,6},{8,11},{9,8},{10,9... | collective-permute-start | bytes 393224 | tf_op jit(solution)/shard_map/ppermute | solution.py:121
  59.5 9.6 %collective-permute-start.12 = (bf16[528,128]{1,0:T(8,128)(2,1)S(1)}, bf16[528,128]{1,0:T(8,128)(2,1)S(1)}, u32[]{:S(2)}, u32[]{:S(2)}) collective-permute-start(bf16[528,128]{1,0:T(8,128)(2,1)S(1)} %shard_map.68), channel_id=1, source_target_pairs={{0,24},{4,28},{8,16},{12,20},{16,8},{20,12},{24,0},{28,4},{1,25},{... | collective-permute-start | bytes 405512 | tf_op jit(solution)/shard_map/ppermute | solution.py:128
  60.9 8.2 %collective-permute-start.11 = (bf16[528,128]{1,0:T(8,128)(2,1)S(1)}, bf16[528,128]{1,0:T(8,128)(2,1)S(1)}, u32[]{:S(2)}, u32[]{:S(2)}) collective-permute-start(bf16[528,128]{1,0:T(8,128)(2,1)S(1)} %shard_map.68), channel_id=1, source_target_pairs={{0,16},{4,20},{8,24},{12,28},{16,0},{20,4},{24,8},{28,12},{1,17},{... | collective-permute-start | bytes 405512 | tf_op jit(solution)/shard_map/ppermute | solution.py:128
  61.5 7.6 %collective-permute-start.10 = (bf16[528,128]{1,0:T(8,128)(2,1)S(1)}, bf16[528,128]{1,0:T(8,128)(2,1)S(1)}, u32[]{:S(2)}, u32[]{:S(2)}) collective-permute-start(bf16[528,128]{1,0:T(8,128)(2,1)S(1)} %shard_map.68), channel_id=1, source_target_pairs={{0,8},{4,12},{8,0},{12,4},{16,24},{20,28},{24,16},{28,20},{1,9},{5... | collective-permute-start | bytes 405512 | tf_op jit(solution)/shard_map/ppermute | solution.py:128
  69.2 9.5 %collective-permute-start.13 = (bf16[4,528,128]{2,1,0:T(8,128)(2,1)S(1)}, bf16[4,528,128]{2,1,0:T(8,128)(2,1)S(1)}, u32[]{:S(2)}, u32[]{:S(2)}) collective-permute-start(bf16[4,528,128]{2,1,0:T(8,128)(2,1)S(1)} %pad_maximum_fusion.1.rest_2_), channel_id=1, source_target_pairs={{0,4},{4,0},{8,12},{12,8},{16,20},{20,16},{24,28},{28,24},{1,5},{5... | collective-permute-start | bytes 1622024 | tf_op jit(solution)/shard_map/ppermute | solution.py:131
  78.7 0.7 copy-start.1
  79.4 0.7 copy-start.2
  (4 other events, 2.5 us)

commit v3 on v2

v3 whole, which is shorter than its diff:
```python
import functools

import jax
import jax.numpy as jnp
from jax import lax
from jax.experimental import pallas as pl
from jax.experimental.pallas import tpu as pltpu
from jax.sharding import PartitionSpec as P

W = 8
SUB = 64
TAPS = 8
TU = 128
NV = 2048
LANES = 128
SUBLANES = 8
BLOCKS = NV // LANES
META = 16
STEP = 4

VMEM = pl.BlockSpec(memory_space=pltpu.VMEM)
SMEM = pl.BlockSpec(memory_space=pltpu.SMEM)
ANY = pl.BlockSpec(memory_space=pl.ANY)


def taper(scaled):
    inner = jnp.maximum(0.0, 1.0 - scaled * scaled)
    return inner * inner


def grid_kernel(values_ref, places_ref, *rest, blanks, orders):
    parts_ref, rest = rest[orders], rest[orders + 1 :]
    zero_copies = []
    if blanks:
        out_ref, values_wide, blank, sem = rest
        blank[...] = jnp.zeros(blank.shape, jnp.float32)
        zero_copies = [pltpu.make_async_copy(blank, out_ref.at[:, plane], sem.at[plane]) for plane in range(W)]
    else:
        (values_wide,) = rest
    for copy in zero_copies:
        copy.start()
    comp_count, sub_count, row_count = values_ref.shape
    peers, _, kept, _ = parts_ref.shape
    for comp in range(comp_count):
        values_wide[comp * sub_count : (comp + 1) * sub_count, :] = values_ref[comp].astype(jnp.float32)
    cells = lax.broadcasted_iota(jnp.int32, (SUB, row_count), 0).astype(jnp.float32) * (2.0 / TAPS)

    def one_sub(sub):
        row_taps = taper(cells - places_ref[0, pl.ds(sub, 1), :] * (2.0 / TAPS)).astype(jnp.bfloat16)
        col_taps = taper(cells - places_ref[1, pl.ds(sub, 1), :] * (2.0 / TAPS))
        weighted = jnp.concatenate(
            [
                (values_wide[pl.ds(comp * sub_count + sub, 1), :] * col_taps).astype(jnp.bfloat16)
                for comp in range(comp_count)
            ],
            axis=0,
        )
        return lax.dot_general(
            weighted, row_taps, (((1,), (1,)), ((), ())), preferred_element_type=jnp.float32
        )

    def some_subs(turn, carry):
        for pair in range(STEP // 2):
            sub = turn * STEP + pair * 2
            sums = jnp.concatenate([one_sub(sub), one_sub(sub + 1)], axis=1).astype(jnp.bfloat16)
            for peer in range(peers):
                parts_ref[peer, turn * (STEP // 2) + pair] = sums[peer * kept : (peer + 1) * kept]
        return carry

    lax.fori_loop(0, sub_count // STEP, some_subs, 0)
    for copy in zero_copies:
        copy.wait()


def grid_parts(values, places, peers, chunk, sub_count, blanks, *order):
    comp_count, _, row_count = values.shape
    kept = comp_count // peers * SUB
    parts_shape = (peers, sub_count // 2, kept, LANES)
    return pl.pallas_call(
        functools.partial(grid_kernel, blanks=blanks, orders=len(order)),
        grid=(1,),
        out_shape=[jax.ShapeDtypeStruct(parts_shape, jnp.bfloat16)]
        + [jax.ShapeDtypeStruct((kept // SUB, W, TU, NV), jnp.float32)] * blanks,
        in_specs=[
            pl.BlockSpec((comp_count, sub_count, row_count), lambda i: (0, chunk, 0)),
            pl.BlockSpec((2, sub_count, row_count), lambda i: (0, chunk, 0)),
        ]
        + [ANY] * len(order),
        out_specs=[pl.BlockSpec(parts_shape, lambda i: (0, 0, 0, 0))] + [ANY] * blanks,
        scratch_shapes=[pltpu.VMEM((comp_count * sub_count, row_count), jnp.float32)]
        + [pltpu.VMEM((kept // SUB, TU, NV), jnp.float32), pltpu.SemaphoreType.DMA((W,))] * blanks,
        compiler_params=pltpu.CompilerParams(vmem_limit_bytes=60 << 20),
        cost_estimate=pl.CostEstimate(
            flops=8 * sub_count * row_count * SUB * SUB * comp_count,
            bytes_accessed=2 << 20,
            transcendentals=0,
        ),
    )(values, places, *order)


def sum_kernel(parts_ref, order_ref, *rest):
    numbers_refs, out_ref = rest[:-1], rest[-1]
    peers, pairs, _, _ = parts_ref.shape
    for pair in range(pairs):
        total = parts_ref[0, pair].astype(jnp.float32)
        for peer in range(1, peers):
            total = total + parts_ref[peer, pair].astype(jnp.float32)
        out_ref[pair * 2 * SUB : (pair + 1) * 2 * SUB, :] = total.T.astype(jnp.bfloat16)
    for numbers_ref in numbers_refs:
        out_ref[pairs * 2 * SUB :, :] = numbers_ref[...].astype(jnp.bfloat16)


def sum_parts(parts, order, *numbers):
    _, pairs, kept, _ = parts.shape
    return pl.pallas_call(
        sum_kernel,
        out_shape=jax.ShapeDtypeStruct((pairs * 2 * SUB + META * len(numbers), kept), jnp.bfloat16),
        in_specs=[VMEM, ANY] + [VMEM] * len(numbers),
        out_specs=VMEM,
        compiler_params=pltpu.CompilerParams(vmem_limit_bytes=8 << 20),
        cost_estimate=pl.CostEstimate(flops=1 << 20, bytes_accessed=2 << 20, transcendentals=0),
    )(parts, order, *numbers)


def gather_all(array, axis):
    size = lax.axis_size(axis)
    near = [array] + [
        lax.ppermute(array, axis, [(i, i ^ mask) for i in range(size)]) for mask in range(2, size, 2)
    ]
    near = jnp.stack(near, axis=0)
    other = lax.ppermute(near, axis, [(i, i ^ 1) for i in range(size)])
    return [near, other]


def touch_plan(starts, planes, cols):
    total = starts.shape[0]
    ids = jnp.arange(total, dtype=jnp.int32)
    taken = starts >= 0
    keys = jnp.where(taken, planes, W) * total + ids
    left = jnp.where(taken, planes * BLOCKS + cols // LANES, -1)
    right = jnp.where(taken & (cols % LANES > LANES - SUB), left + 1, -2)
    before = keys[None, :] < keys[:, None]
    after = keys[None, :] > keys[:, None]
    rank = jnp.sum(before.astype(jnp.int32), axis=1)

    def edges(units):
        same = (left[None, :] == units[:, None]) | (right[None, :] == units[:, None])
        first = ~jnp.any(same & before, axis=1)
        last = ~jnp.any(same & after, axis=1)
        return first.astype(jnp.int32) + 2 * last.astype(jnp.int32)

    flags = edges(left) + jnp.where(right >= 0, 4 * edges(right), 0)
    fields = jnp.stack([starts, cols, planes, ids, flags], axis=0)
    moved = jnp.where(rank[None, None, :] == ids[None, :, None], fields[:, None, :], 0)
    table = jnp.sum(moved, axis=2)
    number = jnp.sum(taken.astype(jnp.int32))
    return jnp.concatenate([table, jnp.full((1, total), number, jnp.int32)], axis=0)


def place_kernel(table_ref, *rest):
    arrays, out_ref, canvas, sem = rest[:-4], rest[-3], rest[-2], rest[-1]
    comp_count = canvas.shape[1]
    blocks = arrays[0].shape[0]
    half = arrays[2].shape[1] // SUB
    sub_count = 2 * half
    lane = lax.broadcasted_iota(jnp.int32, (SUB + SUBLANES, LANES), 1)

    def lanes_of(block):
        return pl.ds(pl.multiple_of(block * LANES, LANES), LANES)

    def out_copy(plane, block):
        return pltpu.make_async_copy(
            canvas.at[plane, :, pl.ds(SUB, TU), lanes_of(block)],
            out_ref.at[:, plane, :, lanes_of(block)],
            sem.at[plane, block],
        )

    def clear(plane, block):
        canvas[plane, :, pl.ds(SUB, TU), lanes_of(block)] = jnp.zeros((comp_count, TU, LANES), jnp.float32)

    def when_set(flags, bit, act):
        @pl.when((flags & bit) != 0)
        def _():
            act()

    def add_patch(index, carry):
        start = table_ref[0, index]
        col = table_ref[1, index]
        plane = table_ref[2, index]
        sub = table_ref[3, index]
        flags = table_ref[4, index]
        block = col // LANES
        shift = col % LANES
        holder = sub // sub_count
        local = sub % sub_count
        source = local // half * 2 + holder // blocks
        at = pl.ds(pl.multiple_of(local % half * SUB, SUB), SUB)

        def from_array(array):
            return lambda: array[holder % blocks, at, :].astype(jnp.float32)

        patch = lax.switch(source, [from_array(array) for array in arrays])
        if patch.shape[1] < LANES:
            patch = jnp.concatenate([patch] * (LANES // patch.shape[1]), axis=1)
        patch = jnp.concatenate([patch, jnp.zeros((SUBLANES, patch.shape[1]), jnp.float32)], axis=0)
        patch = pltpu.roll(patch, start % SUBLANES, 0)
        rows = pl.ds(pl.multiple_of(start // SUBLANES * SUBLANES, SUBLANES), SUB + SUBLANES)
        turned = [
            pltpu.roll(
                patch[:, comp // 2 * LANES : (comp // 2 + 1) * LANES], (shift + comp % 2 * SUB) % LANES, 1
            )
            for comp in range(comp_count)
        ]
        when_set(flags, 1, lambda: clear(plane, block))
        here = (lane >= shift) & (lane < shift + SUB)
        for comp in range(comp_count):
            canvas[plane, comp, rows, lanes_of(block)] += jnp.where(here, turned[comp], 0.0)
        when_set(flags, 2, lambda: out_copy(plane, block).start())

        @pl.when(shift > LANES - SUB)
        def _():
            when_set(flags, 4, lambda: clear(plane, block + 1))
            for comp in range(comp_count):
                canvas[plane, comp, rows, lanes_of(block + 1)] += jnp.where(
                    lane < shift + SUB - LANES, turned[comp], 0.0
                )
            when_set(flags, 8, lambda: out_copy(plane, block + 1).start())

        return carry

    def finish(index, carry):
        block = table_ref[1, index] // LANES
        plane = table_ref[2, index]
        flags = table_ref[4, index]
        when_set(flags, 2, lambda: out_copy(plane, block).wait())
        when_set(flags, 8, lambda: out_copy(plane, block + 1).wait())
        return carry

    lax.fori_loop(0, table_ref[5, 0], add_patch, 0)
    lax.fori_loop(0, table_ref[5, 0], finish, 0)


def place_all(arrays, table, tile_grid):
    comp_count = tile_grid.shape[0]
    return pl.pallas_call(
        place_kernel,
        out_shape=jax.ShapeDtypeStruct(tile_grid.shape, jnp.float32),
        in_specs=[SMEM] + [VMEM] * len(arrays) + [ANY],
        out_specs=ANY,
        scratch_shapes=[
            pltpu.VMEM((W, comp_count, TU + 2 * SUB, NV), jnp.float32),
            pltpu.SemaphoreType.DMA((W, BLOCKS)),
        ],
        input_output_aliases={1 + len(arrays): 0},
        compiler_params=pltpu.CompilerParams(vmem_limit_bytes=44 << 20),
        cost_estimate=pl.CostEstimate(flops=0, bytes_accessed=16 << 20, transcendentals=0),
    )(table, *arrays, tile_grid)


def body(visibilities, positions, owner, w_plane, row_offset, col_offset):
    peers = lax.axis_size("tm")
    tiles = lax.axis_size("uv")
    sub_count = visibilities.shape[1]
    comp_count = visibilities.shape[0] // peers
    kept = comp_count * SUB
    tile = lax.axis_index("uv")
    half = sub_count // 2

    numbers = jnp.stack(
        [owner[:, 0], row_offset, w_plane, col_offset // LANES, col_offset % LANES], axis=0
    ).astype(jnp.float32)
    numbers = jnp.pad(numbers, ((0, META - 5), (0, kept - sub_count)))

    sent_a, tile_grid = grid_parts(visibilities, positions, peers, 0, half, True)
    parts_a = lax.all_to_all(sent_a, "tm", split_axis=0, concat_axis=0, tiled=True)
    (sent_b,) = grid_parts(visibilities, positions, peers, 1, half, False, sent_a)
    parts_b = lax.all_to_all(sent_b, "tm", split_axis=0, concat_axis=0, tiled=True)
    arrays_a = gather_all(sum_parts(parts_a, sent_b, numbers), "uv")

    told = jnp.stack(arrays_a, axis=0)[:, :, half * SUB :, :sub_count].astype(jnp.float32).astype(jnp.int32)
    told = jnp.transpose(told, (2, 0, 1, 3)).reshape(META, -1)
    ahead = (told[0] - tile) % tiles
    starts = jnp.where(ahead == 0, told[1] + SUB, jnp.where(ahead == tiles - 1, told[1] + SUB - TU, -1))
    table = touch_plan(starts, told[2], told[3] * LANES + told[4])
    arrays_b = gather_all(sum_parts(parts_b, arrays_a[1]), "uv")
    return place_all(arrays_a + arrays_b, table, tile_grid)


def solution(mesh):
    placed = (P(None, "uv", "tm"), P(None, "uv", "tm"), P("uv", None), P("uv"), P("uv"), P("uv"))
    return jax.shard_map(
        body, mesh=mesh, in_specs=placed, out_specs=P("tm", None, "uv", None), check_vma=False
    )
```

time: 94 us -> 73.1 us (0.78)
  the two profiles are of different devices: /device:TPU:10 before, /device:TPU:5 now
where the time goes in v3:
time: 73.1 us; the launch traced here: 73.6 us
  Pallas kernels  34.1 us (47%)
  starting transfers between devices  17.1 us (23%)
  waiting for transfers between devices  16.7 us (23%)
  local copies, waits for them, and re-layouts  3.24 us (4%)
  other arithmetic  2.31 us (3%)
    pallas_call x2, Pallas kernels, grid_parts(): pl.pallas_call(functools.partial(grid_kernel, blanks=blanks, orders=len(o...  23.2 us
    pallas_call x1, Pallas kernels, place_all(): pl.pallas_call(place_kernel, out_shape=jax.ShapeDtypeStruct(tile_grid.sha...  10.7 us
    all_to_all x1, waiting for transfers between devices, body(): lax.all_to_all(sent_b, 'tm', split_axis=0, concat_axis=0, tiled=True)  9.48 us
    ppermute x6, starting transfers between devices, gather_all(): lax.ppermute(array, axis, [(i, i ^ mask) for i in range(size)])  5.43 us
    all_to_all x1, starting transfers between devices, body(): lax.all_to_all(sent_a, 'tm', split_axis=0, concat_axis=0, tiled=True)  4.6 us
    ppermute x6, waiting for transfers between devices, gather_all(): lax.ppermute(array, axis, [(i, i ^ mask) for i in range(size)])  4.38 us
    ppermute x2, starting transfers between devices, gather_all(): other = lax.ppermute(near, axis, [(i, i ^ 1) for i in range(size)])  3.57 us
    all_to_all x1, starting transfers between devices, body(): lax.all_to_all(sent_b, 'tm', split_axis=0, concat_axis=0, tiled=True)  3.47 us
  transfers between devices with their start and end apart: 10, of which 6 were waited for; matrix products, arithmetic and copies ran while one was open for 6% of the time, Pallas kernels for 16%

profile of v3, /device:TPU:5, one launch (start us, length us, event | category | flops | bytes accessed | tf_op | source)
XLA Modules:
  0.0 73.6 jit_solution(4198603663816280210)
XLA Ops:
  0.0 11.7 %shard_map.64 = (bf16[4,4,128,128]{3,2,1,0:T(8,128)(2,1)}, f32[2,8,128,2048]{3,2,1,0:T(8,128)}) custom-call(bf16[8,16,4096]{2,1,0:T(8,128)(2,1)} %values_ref.3, f32[2,16,4096]{2,1,0:T(8,128)} %places_ref.3), custom_call_target="tpu_custom_call" | custom-call | flops 8589934592 | bytes 2097152 | tf_op jit(solution)/shard_map/pallas_call | solution.py:79
  11.7 4.6 %all-to-all-start = ((bf16[4,4,128,128]{3,2,1,0:T(8,128)(2,1)}), bf16[4,4,128,128]{3,2,1,0:T(8,128)(2,1)S(1)}, u32[]{:S(2)}, u32[]{:S(2)}) async-start(bf16[4,4,128,128]{3,2,1,0:T(8,128)(2,1)} %get-tuple-element.7.rest_0_), calls=%async_computation | async-start | bytes 1048576 | tf_op jit(solution)/shard_map/all_to_all | solution.py:275
  16.4 11.5 %shard_map.65.order_ref = bf16[4,4,128,128]{3,2,1,0:T(8,128)(2,1)} custom-call(bf16[8,16,4096]{2,1,0:T(8,128)(2,1)} %values_ref.3, f32[2,16,4096]{2,1,0:T(8,128)} %places_ref.3, bf16[4,4,128,128]{3,2,1,0:T(8,128)(2,1)} %get-tuple-element.7.rest_0_), custom_call_target="tpu_custom_call" | custom-call | flops 8589934592 | bytes 2097152 | tf_op jit(solution)/shard_map/pallas_call | solution.py:79
  27.9 2.4 %all-to-all-done.parts_ref = bf16[4,4,128,128]{3,2,1,0:T(8,128)(2,1)S(1)} async-done(((bf16[4,4,128,128]{3,2,1,0:T(8,128)(2,1)}), bf16[4,4,128,128]{3,2,1,0:T(8,128)(2,1)S(1)}, u32[]{:S(2)}, u32[]{:S(2)}) %all-to-all-start) | async-done | bytes 524320 | tf_op jit(solution)/shard_map/all_to_all | solution.py:275
  30.3 1.0 %copy-done = bf16[4,4,128,128]{3,2,1,0:T(8,128)(2,1)S(1)} copy-done((bf16[4,4,128,128]{3,2,1,0:T(8,128)(2,1)S(1)}, bf16[4,4,128,128]{3,2,1,0:T(8,128)(2,1)}, u32[]{:S(2)}) %copy-start) | copy-done | bytes 524312
  31.5 1.2 %collective-permute-start.2 = (bf16[528,128]{1,0:T(8,128)(2,1)S(1)}, bf16[528,128]{1,0:T(8,128)(2,1)S(1)}, u32[]{:S(2)}, u32[]{:S(2)}) collective-permute-start(bf16[528,128]{1,0:T(8,128)(2,1)S(1)} %shard_map.66), channel_id=1, source_target_pairs={{0,24},{4,28},{8,16},{12,20},{16,8},{20,12},{24,0},{28,4},{1,25},{... | collective-permute-start | bytes 405512 | tf_op jit(solution)/shard_map/ppermute | solution.py:128
  32.7 1.2 %collective-permute-start.1 = (bf16[528,128]{1,0:T(8,128)(2,1)S(1)}, bf16[528,128]{1,0:T(8,128)(2,1)S(1)}, u32[]{:S(2)}, u32[]{:S(2)}) collective-permute-start(bf16[528,128]{1,0:T(8,128)(2,1)S(1)} %shard_map.66), channel_id=1, source_target_pairs={{0,16},{4,20},{8,24},{12,28},{16,0},{20,4},{24,8},{28,12},{1,17},{... | collective-permute-start | bytes 405512 | tf_op jit(solution)/shard_map/ppermute | solution.py:128
  34.0 0.3 collective-permute-start
  34.2 3.5 %all-to-all-start.1 = ((bf16[4,4,128,128]{3,2,1,0:T(8,128)(2,1)}), bf16[4,4,128,128]{3,2,1,0:T(8,128)(2,1)S(1)}, u32[]{:S(2)}, u32[]{:S(2)}) async-start(bf16[4,4,128,128]{3,2,1,0:T(8,128)(2,1)} %shard_map.65.order_ref), calls=%async_computation.1 | async-start | bytes 1048576 | tf_op jit(solution)/shard_map/all_to_all | solution.py:277
  37.7 2.4 %collective-permute-done.1 = bf16[528,128]{1,0:T(8,128)(2,1)S(1)} collective-permute-done((bf16[528,128]{1,0:T(8,128)(2,1)S(1)}, bf16[528,128]{1,0:T(8,128)(2,1)S(1)}, u32[]{:S(2)}, u32[]{:S(2)}) %collective-permute-start.1) | collective-permute-done | bytes 135200 | tf_op jit(solution)/shard_map/ppermute | solution.py:128
  40.3 1.3 %collective-permute-start.3 = (bf16[4,528,128]{2,1,0:T(8,128)(2,1)S(1)}, bf16[4,528,128]{2,1,0:T(8,128)(2,1)S(1)}, u32[]{:S(2)}, u32[]{:S(2)}) collective-permute-start(bf16[4,528,128]{2,1,0:T(8,128)(2,1)S(1)} %get-tuple-element.28.rest_0_), channel_id=1, source_target_pairs={{0,4},{4,0},{8,12},{12,8},{16,20},{20,16},{24,28},{28,24},{1,5},{5... | collective-permute-start | bytes 1622024 | tf_op jit(solution)/shard_map/ppermute | solution.py:131
  41.5 9.5 %all-to-all-done.1.parts_ref = bf16[4,4,128,128]{3,2,1,0:T(8,128)(2,1)S(1)} async-done(((bf16[4,4,128,128]{3,2,1,0:T(8,128)(2,1)}), bf16[4,4,128,128]{3,2,1,0:T(8,128)(2,1)S(1)}, u32[]{:S(2)}, u32[]{:S(2)}) %all-to-all-start.1) | async-done | bytes 524320 | tf_op jit(solution)/shard_map/all_to_all | solution.py:277
  51.2 1.2 %collective-permute-start.6 = (bf16[512,128]{1,0:T(8,128)(2,1)S(1)}, bf16[512,128]{1,0:T(8,128)(2,1)S(1)}, u32[]{:S(2)}, u32[]{:S(2)}) collective-permute-start(bf16[512,128]{1,0:T(8,128)(2,1)S(1)} %shard_map.67), channel_id=1, source_target_pairs={{0,24},{4,28},{8,16},{12,20},{16,8},{20,12},{24,0},{28,4},{1,25},{... | collective-permute-start | bytes 393224 | tf_op jit(solution)/shard_map/ppermute | solution.py:128
  52.4 1.2 %collective-permute-start.5 = (bf16[512,128]{1,0:T(8,128)(2,1)S(1)}, bf16[512,128]{1,0:T(8,128)(2,1)S(1)}, u32[]{:S(2)}, u32[]{:S(2)}) collective-permute-start(bf16[512,128]{1,0:T(8,128)(2,1)S(1)} %shard_map.67), channel_id=1, source_target_pairs={{0,16},{4,20},{8,24},{12,28},{16,0},{20,4},{24,8},{28,12},{1,17},{... | collective-permute-start | bytes 393224 | tf_op jit(solution)/shard_map/ppermute | solution.py:128
  53.6 0.3 collective-permute-start.4
  53.9 0.6 broadcast.901
  54.5 1.5 %fusion.22 = (s32[2,4,16]{2,1,0:T(4,128)S(1)}, s32[1,2,4,16]{3,0,2,1:T(1,128)S(1)}, s32[1,2,4,16]{3,0,2,1:T(1,128)S(1)}, s32[1,2,4,16]{3,0,2,1:T(1,128)S(1)}, s3...) fusion(s32[]{:T(128)} %broadcast.901, ...), kind=kLoop, calls=%fused_computation.79 | loop fusion | flops 2943 | bytes 7692 | tf_op jit(solution)/shard_map/add | solution.py:284
  56.8 0.2 fusion.1
  57.1 0.8 %collective-permute-done.5 = bf16[512,128]{1,0:T(8,128)(2,1)S(1)} collective-permute-done((bf16[512,128]{1,0:T(8,128)(2,1)S(1)}, bf16[512,128]{1,0:T(8,128)(2,1)S(1)}, u32[]{:S(2)}, u32[]{:S(2)}) %collective-permute-start.5) | collective-permute-done | bytes 131104 | tf_op jit(solution)/shard_map/ppermute | solution.py:128
  57.9 1.2 %collective-permute-done.4 = bf16[512,128]{1,0:T(8,128)(2,1)S(1)} collective-permute-done((bf16[512,128]{1,0:T(8,128)(2,1)S(1)}, bf16[512,128]{1,0:T(8,128)(2,1)S(1)}, u32[]{:S(2)}, u32[]{:S(2)}) %collective-permute-start.4) | collective-permute-done | bytes 131104 | tf_op jit(solution)/shard_map/ppermute | solution.py:128
  59.1 2.3 %collective-permute-start.7 = (bf16[4,512,128]{2,1,0:T(8,128)(2,1)S(1)}, bf16[4,512,128]{2,1,0:T(8,128)(2,1)S(1)}, u32[]{:S(2)}, u32[]{:S(2)}) collective-permute-start(bf16[4,512,128]{2,1,0:T(8,128)(2,1)S(1)} %pad_maximum_fusion.1.rest_2_), channel_id=1, source_target_pairs={{0,4},{4,0},{8,12},{12,8},{16,20},{20,16},{24,28},{28,24},{1,5},{5... | collective-permute-start | bytes 1572872 | tf_op jit(solution)/shard_map/ppermute | solution.py:131
  61.8 0.7 concatenate.3.table_ref
  62.5 0.4 collective-permute-done.7.rest_3_
  62.9 10.7 %shard_map.68 = f32[2,8,128,2048]{3,2,1,0:T(8,128)} custom-call(s32[6,128]{1,0:T(8,128)S(1)} %concatenate.3.table_ref, bf16[4,528,128]{2,1,0:T(8,128)(2,1)S(1)} %get-tuple-element.28.rest_0_, bf16[4,528,128]{2,1,0:T(8,128)(2,1)S(1)} %collective-permute-done.3.order_ref.rest_1_, ...), custom_call_target="tpu_custom_call", output_to_operand_aliasing={{}: (5, {})} | custom-call | bytes 16777216 | tf_op jit(solution)/shard_map/pallas_call | solution.py:245
  (40 shorter events, 1.8 us)
Async XLA Ops:
  0.0 16.3 %copy-start.4 = (s32[16]{0:T(128)S(1)}, s32[16]{0:T(128)}, u32[]{:S(2)}) copy-start(s32[16]{0:T(128)} %param.11) | copy-start | bytes 196
  0.0 16.4 %copy-start.2 = (s32[16]{0:T(128)S(1)}, s32[16]{0:T(128)}, u32[]{:S(2)}) copy-start(s32[16]{0:T(128)} %param.10) | copy-start | bytes 196
  0.0 16.4 %copy-start.3 = (s32[16]{0:T(128)S(1)}, s32[16]{0:T(128)}, u32[]{:S(2)}) copy-start(s32[16]{0:T(128)} %param.9) | copy-start | bytes 196
  0.0 16.4 %copy-start.1 = (s32[16,1]{0,1:T(1,128)S(1)}, s32[16,1]{0,1:T(1,128)}, u32[]{:S(2)}) copy-start(s32[16,1]{0,1:T(1,128)} %param.8) | copy-start | bytes 196
  11.7 18.6 %all-to-all-start = ((bf16[4,4,128,128]{3,2,1,0:T(8,128)(2,1)}), bf16[4,4,128,128]{3,2,1,0:T(8,128)(2,1)S(1)}, u32[]{:S(2)}, u32[]{:S(2)}) async-start(bf16[4,4,128,128]{3,2,1,0:T(8,128)(2,1)} %get-tuple-element.7.rest_0_), calls=%async_computation | async-start | bytes 1048576 | tf_op jit(solution)/shard_map/all_to_all | solution.py:275
  30.3 1.0 %copy-start = (bf16[4,4,128,128]{3,2,1,0:T(8,128)(2,1)S(1)}, bf16[4,4,128,128]{3,2,1,0:T(8,128)(2,1)}, u32[]{:S(2)}) copy-start(bf16[4,4,128,128]{3,2,1,0:T(8,128)(2,1)} %shard_map.65.order_ref) | copy-start | bytes 1572868
  31.5 6.2 %collective-permute-start.2 = (bf16[528,128]{1,0:T(8,128)(2,1)S(1)}, bf16[528,128]{1,0:T(8,128)(2,1)S(1)}, u32[]{:S(2)}, u32[]{:S(2)}) collective-permute-start(bf16[528,128]{1,0:T(8,128)(2,1)S(1)} %shard_map.66), channel_id=1, source_target_pairs={{0,24},{4,28},{8,16},{12,20},{16,8},{20,12},{24,0},{28,4},{1,25},{... | collective-permute-start | bytes 405512 | tf_op jit(solution)/shard_map/ppermute | solution.py:128
  32.7 7.4 %collective-permute-start.1 = (bf16[528,128]{1,0:T(8,128)(2,1)S(1)}, bf16[528,128]{1,0:T(8,128)(2,1)S(1)}, u32[]{:S(2)}, u32[]{:S(2)}) collective-permute-start(bf16[528,128]{1,0:T(8,128)(2,1)S(1)} %shard_map.66), channel_id=1, source_target_pairs={{0,16},{4,20},{8,24},{12,28},{16,0},{20,4},{24,8},{28,12},{1,17},{... | collective-permute-start | bytes 405512 | tf_op jit(solution)/shard_map/ppermute | solution.py:128
  34.0 6.2 %collective-permute-start = (bf16[528,128]{1,0:T(8,128)(2,1)S(1)}, bf16[528,128]{1,0:T(8,128)(2,1)S(1)}, u32[]{:S(2)}, u32[]{:S(2)}) collective-permute-start(bf16[528,128]{1,0:T(8,128)(2,1)S(1)} %shard_map.66), channel_id=1, source_target_pairs={{0,8},{4,12},{8,0},{12,4},{16,24},{20,28},{24,16},{28,20},{1,9},{5... | collective-permute-start | bytes 405512 | tf_op jit(solution)/shard_map/ppermute | solution.py:128
  34.2 16.8 %all-to-all-start.1 = ((bf16[4,4,128,128]{3,2,1,0:T(8,128)(2,1)}), bf16[4,4,128,128]{3,2,1,0:T(8,128)(2,1)S(1)}, u32[]{:S(2)}, u32[]{:S(2)}) async-start(bf16[4,4,128,128]{3,2,1,0:T(8,128)(2,1)} %shard_map.65.order_ref), calls=%async_computation.1 | async-start | bytes 1048576 | tf_op jit(solution)/shard_map/all_to_all | solution.py:277
  40.3 10.8 %collective-permute-start.3 = (bf16[4,528,128]{2,1,0:T(8,128)(2,1)S(1)}, bf16[4,528,128]{2,1,0:T(8,128)(2,1)S(1)}, u32[]{:S(2)}, u32[]{:S(2)}) collective-permute-start(bf16[4,528,128]{2,1,0:T(8,128)(2,1)S(1)} %get-tuple-element.28.rest_0_), channel_id=1, source_target_pairs={{0,4},{4,0},{8,12},{12,8},{16,20},{20,16},{24,28},{28,24},{1,5},{5... | collective-permute-start | bytes 1622024 | tf_op jit(solution)/shard_map/ppermute | solution.py:131
  51.2 5.9 %collective-permute-start.6 = (bf16[512,128]{1,0:T(8,128)(2,1)S(1)}, bf16[512,128]{1,0:T(8,128)(2,1)S(1)}, u32[]{:S(2)}, u32[]{:S(2)}) collective-permute-start(bf16[512,128]{1,0:T(8,128)(2,1)S(1)} %shard_map.67), channel_id=1, source_target_pairs={{0,24},{4,28},{8,16},{12,20},{16,8},{20,12},{24,0},{28,4},{1,25},{... | collective-permute-start | bytes 393224 | tf_op jit(solution)/shard_map/ppermute | solution.py:128
  52.4 5.5 %collective-permute-start.5 = (bf16[512,128]{1,0:T(8,128)(2,1)S(1)}, bf16[512,128]{1,0:T(8,128)(2,1)S(1)}, u32[]{:S(2)}, u32[]{:S(2)}) collective-permute-start(bf16[512,128]{1,0:T(8,128)(2,1)S(1)} %shard_map.67), channel_id=1, source_target_pairs={{0,16},{4,20},{8,24},{12,28},{16,0},{20,4},{24,8},{28,12},{1,17},{... | collective-permute-start | bytes 393224 | tf_op jit(solution)/shard_map/ppermute | solution.py:128
  53.6 5.4 %collective-permute-start.4 = (bf16[512,128]{1,0:T(8,128)(2,1)S(1)}, bf16[512,128]{1,0:T(8,128)(2,1)S(1)}, u32[]{:S(2)}, u32[]{:S(2)}) collective-permute-start(bf16[512,128]{1,0:T(8,128)(2,1)S(1)} %shard_map.67), channel_id=1, source_target_pairs={{0,8},{4,12},{8,0},{12,4},{16,24},{20,28},{24,16},{28,20},{1,9},{5... | collective-permute-start | bytes 393224 | tf_op jit(solution)/shard_map/ppermute | solution.py:128
  59.1 3.8 %collective-permute-start.7 = (bf16[4,512,128]{2,1,0:T(8,128)(2,1)S(1)}, bf16[4,512,128]{2,1,0:T(8,128)(2,1)S(1)}, u32[]{:S(2)}, u32[]{:S(2)}) collective-permute-start(bf16[4,512,128]{2,1,0:T(8,128)(2,1)S(1)} %pad_maximum_fusion.1.rest_2_), channel_id=1, source_target_pairs={{0,4},{4,0},{8,12},{12,8},{16,20},{20,16},{24,28},{28,24},{1,5},{5... | collective-permute-start | bytes 1572872 | tf_op jit(solution)/shard_map/ppermute | solution.py:131
